TPU v7x, 128 devices: a whole 4x4x4 slice. The times are simulated.
128 devices in a mesh: dst: 64 (over x, z, y_lo, core), tok: 2 (over y_hi).
Axes of the slice: x: 4, y: 4 (y_hi: 2, y_lo: 2; y = y_hi * 2 + y_lo), z: 4, core: 2. Of those that a mesh axis runs over, the one named last changes fastest.
Arguments:
- latents: float32 [2048, 32768], P('tok', 'dst'), may hold values from 0 to 0.2, as said below
- mask: int32 [2048, 32768], P('tok', 'dst'), may hold values from 0 to 1
- errors: bfloat16 [2048, 4, 2048], P('tok'), may hold values from -6 to 6
- decoder: bfloat16 [32768, 4, 2048], P('dst'), may hold values from -0.125 to 0.125
Outputs:
- decoder_grad: bfloat16 [32768, 4, 2048], P('dst', None, 'tok')
- latent_grad: float32 [2048, 32768], P('tok', 'dst')
Inputs may be any that keep to these rules, and one draw needn't show every extreme that they name: `latents`: zero exactly where mask is 0 and positive where mask is 1.
All inputs are finite; a program needn't handle non-finite values.
Results may differ from a plain program's by a relative error of at most 0.001.
Values may be sent and summed in bfloat16 or wider, within the bound.
No kernel may reach another device: no remote copies, remote signals or barrier semaphores. Data moves between devices by JAX's collectives and lax.ppermute only.
A program may use at most 192 MiB of HBM per device.

v0:
```python
import jax
import jax.numpy as jnp
from jax import lax
from jax.experimental import pallas as pl
from jax.experimental.pallas import tpu as pltpu
from jax.sharding import PartitionSpec as P


LAYERS = 4
BF = jnp.bfloat16
F32 = jnp.float32
I16 = jnp.int16
SCALE_ROWS = 16


def params(mib=60):
    return pltpu.CompilerParams(vmem_limit_bytes=mib << 20)


def cost(flops, moved):
    return pl.CostEstimate(flops=flops, bytes_accessed=moved, transcendentals=0)


def picker(tokens, layers):
    row = lax.broadcasted_iota(jnp.int32, (len(layers) * tokens, LAYERS * tokens), 0)
    col = lax.broadcasted_iota(jnp.int32, (len(layers) * tokens, LAYERS * tokens), 1)
    hit = None
    for i, layer in enumerate(layers):
        one = (row >= i * tokens) & (row < (i + 1) * tokens) & (col == (row - i * tokens) * LAYERS + layer)
        hit = one if hit is None else hit | one
    return hit.astype(F32).astype(BF)


def split_transposed(block):
    wide = block.T
    high = wide.astype(BF)
    low = (wide - high.astype(F32)).astype(BF)
    return jnp.concatenate([high, low], axis=1)


def encode(values, out):
    rows = values.shape[0]
    top = jnp.maximum(jnp.max(jnp.abs(values), axis=0, keepdims=True), 1e-30)
    power = jnp.ceil(jnp.log2(top))
    coded = jnp.clip(jnp.round(values * jnp.exp2(15 - power)), -32767, 32767)
    out[:rows] = coded.astype(jnp.int32).astype(I16)
    power = jnp.broadcast_to(power, (SCALE_ROWS, values.shape[1]))
    out[rows:] = power.astype(jnp.int32).astype(I16)


def wide(block):
    return block.astype(jnp.int32).astype(F32)


def unit(scales):
    return jnp.exp2(wide(scales)[:1] - 15)


SUB = 64


def first_kernel(idx, er, lat, own_e, l_code, a_code, a_keep, o_code, o_keep, pick, e_a, a_send, o_send):
    step = pl.program_id(0)
    tokens, _, width = er.shape
    half = width // 2
    last = step == pl.num_programs(0) - 1
    early = idx[0] < LAYERS - 1

    @pl.when(step == 0)
    def _():
        pick[...] = picker(SUB, [idx[0], idx[1]])

    for j in range(tokens // SUB):
        rows = er[j * SUB : (j + 1) * SUB].reshape(LAYERS * SUB, width)
        got = jnp.dot(pick[...], rows, preferred_element_type=F32).astype(BF)
        own_e[j * SUB : (j + 1) * SUB] = got[:SUB]
        e_a[j * SUB : (j + 1) * SUB] = got[SUB:]
    left = split_transposed(lat[pl.ds(pl.multiple_of(step * tokens, tokens), tokens)])
    keep_at = pl.multiple_of(idx[2] * half, half)
    send_at = pl.multiple_of((1 - idx[2]) * half, half)

    def add(out, source, start):
        right = source[:, pl.ds(start, half)]
        term = jnp.dot(left, jnp.concatenate([right, right], axis=0), preferred_element_type=F32)
        out[...] = term + jnp.where(step > 0, out[...], 0.0)

    add(o_send, own_e, send_at)
    add(o_keep, own_e, keep_at)

    @pl.when(early)
    def _():
        add(a_send, e_a, send_at)
        add(a_keep, e_a, keep_at)

    @pl.when(last & early)
    def _():
        encode(a_send[...], a_code)

    @pl.when(last)
    def _():
        encode(o_send[...], o_code)

    @pl.when(last & (idx[0] < 2))
    def _():
        encode(lat[...], l_code)


def first_terms(idx, errors, latents, tile=256):
    tokens, _, width = errors.shape
    f = latents.shape[1]
    half = width // 2
    whole = pl.BlockSpec((f, half), lambda i, s: (0, 0))
    whole_code = pl.BlockSpec((f + SCALE_ROWS, half), lambda i, s: (0, 0))
    shape = jax.ShapeDtypeStruct((f, half), F32)
    code = jax.ShapeDtypeStruct((f + SCALE_ROWS, half), I16)
    return pl.pallas_call(
        first_kernel,
        name="first_terms",
        grid_spec=pltpu.PrefetchScalarGridSpec(
            num_scalar_prefetch=1,
            grid=(tokens // tile,),
            in_specs=[
                pl.BlockSpec((tile, LAYERS, width), lambda i, s: (i, 0, 0)),
                pl.BlockSpec((tokens, f), lambda i, s: (0, 0)),
            ],
            out_specs=[
                pl.BlockSpec((tile, width), lambda i, s: (i, 0)),
                pl.BlockSpec((tokens + SCALE_ROWS, f), lambda i, s: (0, 0)),
                whole_code,
                whole,
                whole_code,
                whole,
            ],
            scratch_shapes=[
                pltpu.VMEM((2 * SUB, LAYERS * SUB), BF),
                pltpu.VMEM((tile, width), BF),
                pltpu.VMEM((f, half), F32),
                pltpu.VMEM((f, half), F32),
            ],
        ),
        out_shape=[
            jax.ShapeDtypeStruct((tokens, width), BF),
            jax.ShapeDtypeStruct((tokens + SCALE_ROWS, f), I16),
            code,
            shape,
            code,
            shape,
        ],
        compiler_params=params(),
        cost_estimate=cost(16 * tokens * f * width, 30 << 20),
    )(idx, errors, latents)


def more_kernel(idx, near, far, e, a_keep, a_come, a_scale, a_done, code, keep, left):
    step = pl.program_id(0)
    rows = near.shape[0] - SCALE_ROWS
    late = idx[0] > 0
    a_done[...] = (a_keep[...] + wide(a_come[...]) * unit(a_scale[...])).astype(BF)

    @pl.when((step == 0) & late)
    def _():
        both = near[...].astype(jnp.int32) + far[...].astype(jnp.int32)
        left[...] = split_transposed(both[:rows].astype(F32) * jnp.exp2(both[rows : rows + 1].astype(F32) - 15))

    def term():
        right = e[...]
        return jnp.dot(left[...], jnp.concatenate([right, right], axis=0), preferred_element_type=F32)

    @pl.when((step < 2) & late)
    def _():
        encode(term(), code)

    @pl.when((step >= 2) & late)
    def _():
        keep[...] = term()


def more_terms(idx, near, far, e, a_keep, a_come):
    rows, f = near.shape
    tokens, width = e.shape
    tile = width // 4
    half = width // 2
    part = pl.BlockSpec((f // 4, half), lambda i, s: (i, 0))
    return pl.pallas_call(
        more_kernel,
        name="more_terms",
        grid_spec=pltpu.PrefetchScalarGridSpec(
            num_scalar_prefetch=1,
            grid=(4,),
            in_specs=[
                pl.BlockSpec((rows, f), lambda i, s: (0, 0)),
                pl.BlockSpec((rows, f), lambda i, s: (0, 0)),
                pl.BlockSpec((tokens, tile), lambda i, s: (0, lax.rem(i + 2 * (1 - s[2]), 4))),
                part,
                part,
                pl.BlockSpec((SCALE_ROWS, half), lambda i, s: (f // SCALE_ROWS, 0)),
            ],
            out_specs=[
                part,
                pl.BlockSpec((f + SCALE_ROWS, tile), lambda i, s: (0, jnp.minimum(i, 1))),
                pl.BlockSpec((f, tile), lambda i, s: (0, jnp.maximum(i - 2, 0))),
            ],
            scratch_shapes=[pltpu.VMEM((f, 2 * tokens), BF)],
        ),
        out_shape=[
            jax.ShapeDtypeStruct((f, half), BF),
            jax.ShapeDtypeStruct((f + SCALE_ROWS, half), I16),
            jax.ShapeDtypeStruct((f, half), F32),
        ],
        compiler_params=params(40),
        cost_estimate=cost(4 * tokens * f * width, 12 << 20),
    )(idx, near, far, e, a_keep, a_come, a_come)


W_SUB = 64


def partial_kernel(idx, e, w, own, one, two, three, pick, plain):
    f, _, width = w.shape

    @pl.when(pl.program_id(0) == 0)
    def _():
        pick[...] = picker(W_SUB, [0, 1, 2, 3])

    for j in range(f // W_SUB):
        rows = w[j * W_SUB : (j + 1) * W_SUB].reshape(LAYERS * W_SUB, width)
        got = jnp.dot(pick[...], rows, preferred_element_type=F32).astype(BF)
        for k in range(LAYERS):
            plain[k * f + j * W_SUB : k * f + (j + 1) * W_SUB] = got[k * W_SUB : (k + 1) * W_SUB]

    for place in range(LAYERS):

        @pl.when(idx[0] == place)
        def _():
            rows = plain[: (place + 1) * f]
            terms = lax.dot_general(e[...], rows, (((1,), (1,)), ((), ())), preferred_element_type=F32)
            own[...] = terms[:, :f]
            for k, code in ((1, one), (2, two), (3, three))[:place]:
                encode(terms[:, k * f : (k + 1) * f], code)


def partials(idx, e, decoder):
    tokens, width = e.shape
    f = decoder.shape[0]
    tile = 128
    code = pl.BlockSpec((tokens + SCALE_ROWS, tile), lambda i, s: (0, i))
    return pl.pallas_call(
        partial_kernel,
        name="partials",
        grid_spec=pltpu.PrefetchScalarGridSpec(
            num_scalar_prefetch=1,
            grid=(f // tile,),
            in_specs=[
                pl.BlockSpec((tokens, width), lambda i, s: (0, 0)),
                pl.BlockSpec((tile, LAYERS, width), lambda i, s: (i, 0, 0)),
            ],
            out_specs=[pl.BlockSpec((tokens, tile), lambda i, s: (0, i)), code, code, code],
            scratch_shapes=[
                pltpu.VMEM((LAYERS * W_SUB, LAYERS * W_SUB), BF),
                pltpu.VMEM((LAYERS * tile, width), BF),
            ],
        ),
        out_shape=[jax.ShapeDtypeStruct((tokens, f), F32)] + [jax.ShapeDtypeStruct((tokens + SCALE_ROWS, f), I16)] * 3,
        compiler_params=params(40),
        cost_estimate=cost(8 * tokens * f * width, 20 << 20),
    )(idx, e, decoder)


WEAVE = 64


def weave_kernel(idx, o_keep, o_come, o_scale, b_keep, b_come, b_scale, r_a, r_b, out, mix):
    f, width = o_keep.shape
    place = idx[0]

    @pl.when(pl.program_id(0) == 0)
    def _():
        row = lax.broadcasted_iota(jnp.int32, (LAYERS * WEAVE, LAYERS * WEAVE), 0)
        col = lax.broadcasted_iota(jnp.int32, (LAYERS * WEAVE, LAYERS * WEAVE), 1)
        mix[...] = (col == (row % LAYERS) * WEAVE + row // LAYERS).astype(F32).astype(BF)

    zero = jnp.zeros((WEAVE, width), BF)
    for j in range(f // WEAVE):
        part = slice(j * WEAVE, (j + 1) * WEAVE)
        own = (o_keep[part] + wide(o_come[part]) * unit(o_scale[...])).astype(BF)
        slot_b = (b_keep[part] + wide(b_come[part]) * unit(b_scale[...])).astype(BF)
        one = jnp.where(place == 0, zero, jnp.where(place == 3, r_b[part], slot_b))
        two = jnp.where(place >= 2, r_a[part], zero)
        three = jnp.where(place == 3, slot_b, zero)
        rows = jnp.concatenate([own, one, two, three], axis=0)
        out[part] = jnp.dot(mix[...], rows, preferred_element_type=F32).astype(BF).reshape(WEAVE, LAYERS, width)


def weave(idx, o_keep, o_come, b_keep, b_come, r_a, r_b):
    f, width = o_keep.shape
    tile = 256
    block = pl.BlockSpec((tile, width), lambda i, s: (i, 0))
    scale = pl.BlockSpec((SCALE_ROWS, width), lambda i, s: (f // SCALE_ROWS, 0))
    return pl.pallas_call(
        weave_kernel,
        name="weave",
        grid_spec=pltpu.PrefetchScalarGridSpec(
            num_scalar_prefetch=1,
            grid=(f // tile,),
            in_specs=[block, block, scale, block, block, scale, block, block],
            out_specs=pl.BlockSpec((tile, LAYERS, width), lambda i, s: (i, 0, 0)),
            scratch_shapes=[pltpu.VMEM((LAYERS * WEAVE, LAYERS * WEAVE), BF)],
        ),
        out_shape=jax.ShapeDtypeStruct((f, LAYERS, width), BF),
        compiler_params=params(36),
        cost_estimate=cost(2 * f * LAYERS * 256 * width, 8 << 20),
    )(idx, o_keep, o_come, o_come, b_keep, b_come, b_come, r_a, r_b)


def moved(array, group, pairs):
    return lax.ppermute(array, "dst", [(a * group + i, b * group + i) for a, b in pairs for i in range(group)])


def swapped(array):
    return lax.ppermute(array, "tok", [(0, 1), (1, 0)])


def gate_kernel(mask, own, one, two, three, one_scale, two_scale, three_scale, out):
    total = own[...]
    for code, scale in ((one, one_scale), (two, two_scale), (three, three_scale)):
        total = total + wide(code[...]) * unit(scale[...])
    out[...] = mask[...].astype(F32) * total


def gated(mask, own, terms):
    tokens, f = own.shape
    tile = 512
    block = pl.BlockSpec((tile, f), lambda i: (i, 0))
    scale = pl.BlockSpec((SCALE_ROWS, f), lambda i: (tokens // SCALE_ROWS, 0))
    return pl.pallas_call(
        gate_kernel,
        name="gate",
        grid=(tokens // tile,),
        in_specs=[block] * 5 + [scale] * 3,
        out_specs=block,
        out_shape=jax.ShapeDtypeStruct((tokens, f), F32),
        compiler_params=params(30),
        cost_estimate=cost(8 * tokens * f, 9 << 20),
    )(mask, own, *terms, *terms)


def after(array, earlier):
    return lax.optimization_barrier((array, earlier))[0]


def per_device(latents, mask, errors, decoder):
    group = lax.axis_size("dst") // LAYERS
    place = lax.axis_index("dst") // group
    other = jnp.where(place == 0, 2, 3)
    idx = jnp.stack([place, other, lax.axis_index("tok")]).astype(jnp.int32)

    own_e, l_code, a_code, a_keep, o_code, o_keep = first_terms(idx, errors, latents)
    a_come = swapped(a_code)
    o_come = swapped(o_code)
    near = moved(l_code, group, [(0, 1), (1, 2)])
    far = moved(l_code, group, [(0, 3)])

    own_p, one_p, two_p, three_p = partials(idx, own_e, decoder)
    three = moved(three_p, group, [(3, 0)])
    two = moved(two_p, group, [(3, 1), (2, 0)])
    one = moved(one_p, group, [(3, 2), (2, 1), (1, 0)])

    a_done, b_code, b_keep = more_terms(idx, after(near, own_p), far, own_e, a_keep, a_come)
    b_come = swapped(b_code)
    r_a = moved(a_done, group, [(0, 2), (1, 3)])
    r_b = moved(a_done, group, [(2, 3)])

    latent_grad = gated(after(mask, b_code), own_p, (one, two, three))
    decoder_grad = weave(idx, after(o_keep, latent_grad), o_come, b_keep, b_come, r_a, r_b)
    return decoder_grad, latent_grad


def solution(mesh):
    placed = (P("tok", "dst"), P("tok", "dst"), P("tok", None, None), P("dst", None, None))
    return jax.shard_map(
        per_device,
        mesh=mesh,
        in_specs=placed,
        out_specs=(P("dst", None, "tok"), P("tok", "dst")),
        check_vma=False,
    )
```

profile of v0, /device:TPU:38, one launch (start us, length us, event | category | flops | bytes accessed | tf_op | source)
XLA Modules:
  0.0 125.6 jit_solution(17997041110054058965)
XLA Ops:
  0.6 0.6 pad_add_fusion.idx
  1.2 16.5 %first_terms.1 = (bf16[1024,2048]{1,0:T(8,128)(2,1)}, s16[1040,512]{1,0:T(8,128)(2,1)}, s16[528,1024]{1,0:T(8,128)(2,1)}, f32[512,1024]{1,0:T(8,128)}, s16[528,1024]{1,0:T(8,128)(2,1)}, /*index=5*/f32[512,1024]{1,0:T(8,128)}) custom-call(s32[3]{0:T(128)} %pad_add_fusion.idx, bf16[1024,4,2048]{2,1,0:T(4,128)(2,1)} %er.1, f32[1024,512]{1,0:T(8,128)} %lat.1), custom_call_target="tpu_custom_call" | custom-call | flops 17179869184 | bytes 31457280 | tf_op jit(solution)/shard_map/first_terms/pallas_call | solution.py:116
  17.8 1.3 %collective-permute-start.1 = (s16[1040,512]{1,0:T(8,128)(2,1)}, s16[1040,512]{1,0:T(8,128)(2,1)S(1)}, u32[]{:S(2)}, u32[]{:S(2)}) collective-permute-start(s16[1040,512]{1,0:T(8,128)(2,1)} %get-tuple-element.19), channel_id=1, source_target_pairs={{0,96},{2,98},{4,100},{6,102},{8,104},{10,106},{12,108},{14,110},{... | collective-permute-start | bytes 3194888 | tf_op jit(solution)/shard_map/ppermute | solution.py:316
  19.1 0.7 collective-permute-start
  19.8 3.3 %collective-permute-start.2 = (s16[528,1024]{1,0:T(8,128)(2,1)}, s16[528,1024]{1,0:T(8,128)(2,1)S(1)}, u32[]{:S(2)}, u32[]{:S(2)}) collective-permute-start(s16[528,1024]{1,0:T(8,128)(2,1)} %get-tuple-element.24), channel_id=1, source_target_pairs={{0,1},{1,0},{2,3},{3,2},{4,5},{5,4},{6,7},{7,6},{8,9},{9,8},{10,11... | collective-permute-start | bytes 3244040 | tf_op jit(solution)/shard_map/ppermute | solution.py:320
  23.1 2.2 %copy-done.7 = bf16[1024,2048]{1,0:T(8,128)(2,1)S(1)} copy-done((bf16[1024,2048]{1,0:T(8,128)(2,1)S(1)}, bf16[1024,2048]{1,0:T(8,128)(2,1)}, u32[]{:S(2)}) %copy-start.7) | copy-done | bytes 4194328
  25.2 16.8 %partials.1 = (f32[1024,512]{1,0:T(8,128)S(1)}, s16[1040,512]{1,0:T(8,128)(2,1)S(1)}, s16[1040,512]{1,0:T(8,128)(2,1)S(1)}, s16[1040,512]{1,0:T(8,128)(2,1)S(1)}) custom-call(s32[3]{0:T(128)S(1)} %copy-done.2, bf16[1024,2048]{1,0:T(8,128)(2,1)S(1)} %copy-done.7, bf16[512,4,2048]{2,1,0:T(4,128)(2,1)} %w.1), custom_call_target="tpu_custom_call" | custom-call | flops 8589934592 | bytes 20971520 | tf_op jit(solution)/shard_map/partials/pallas_call | solution.py:247
  42.1 7.3 %collective-permute-start.3 = (s16[1040,512]{1,0:T(8,128)(2,1)S(1)}, s16[1040,512]{1,0:T(8,128)(2,1)S(1)}, u32[]{:S(2)}, u32[]{:S(2)}) collective-permute-start(s16[1040,512]{1,0:T(8,128)(2,1)S(1)} %get-tuple-element.27), channel_id=1, source_target_pairs={{96,64},{98,66},{100,68},{102,70},{104,72},{106,74},{108,76},{110,... | collective-permute-start | bytes 3194888 | tf_op jit(solution)/shard_map/ppermute | solution.py:316
  49.4 1.5 %collective-permute-start.4 = (s16[1040,512]{1,0:T(8,128)(2,1)S(1)}, s16[1040,512]{1,0:T(8,128)(2,1)S(1)}, u32[]{:S(2)}, u32[]{:S(2)}) collective-permute-start(s16[1040,512]{1,0:T(8,128)(2,1)S(1)} %get-tuple-element.28), channel_id=1, source_target_pairs={{96,32},{98,34},{100,36},{102,38},{104,40},{106,42},{108,44},{110,... | collective-permute-start | bytes 3194888 | tf_op jit(solution)/shard_map/ppermute | solution.py:316
  51.0 0.0 collective-permute-done.near
  51.0 0.0 copy-start.5
  51.0 1.0 copy-done.5
  51.9 0.3 collective-permute-start.6
  52.3 0.0 collective-permute-done.1.far
  52.3 1.0 copy-done.3
  53.3 0.0 collective-permute-done.2.a_come.a_scale
  53.3 1.2 copy-done.4
  54.5 1.2 copy-done.6
  55.8 1.6 %copy-done.8 = f32[512,1024]{1,0:T(8,128)S(1)} copy-done((f32[512,1024]{1,0:T(8,128)S(1)}, f32[512,1024]{1,0:T(8,128)}, u32[]{:S(2)}) %copy-start.8) | copy-done | bytes 2097176
  57.4 7.8 %more_terms.1 = (bf16[512,1024]{1,0:T(8,128)(2,1)S(1)}, s16[528,1024]{1,0:T(8,128)(2,1)S(1)}, f32[512,1024]{1,0:T(8,128)S(1)}) custom-call(s32[3]{0:T(128)S(1)} %copy-done.2, s16[1040,512]{1,0:T(8,128)(2,1)S(1)} %copy-done.6, s16[1040,512]{1,0:T(8,128)(2,1)S(1)} %copy-done.4, bf16[1024,2048]{1,0:T(8,128)(2,1)S(1)} %copy-done.7, f32[512,1024]{1,0:T(8,128)S(1)} %copy-done.8, ...), custom_call_target="tpu_custom_call" | custom-call | flops 4294967296 | bytes 12582912 | tf_op jit(solution)/shard_map/more_terms/pallas_call | solution.py:184
  65.2 3.3 %collective-permute-start.7 = (s16[528,1024]{1,0:T(8,128)(2,1)S(1)}, s16[528,1024]{1,0:T(8,128)(2,1)S(1)}, u32[]{:S(2)}, u32[]{:S(2)}) collective-permute-start(s16[528,1024]{1,0:T(8,128)(2,1)S(1)} %get-tuple-element.25), channel_id=1, source_target_pairs={{0,1},{1,0},{2,3},{3,2},{4,5},{5,4},{6,7},{7,6},{8,9},{9,8},{10,11... | collective-permute-start | bytes 3244040 | tf_op jit(solution)/shard_map/ppermute | solution.py:320
  68.4 1.3 %collective-permute-start.5 = (s16[1040,512]{1,0:T(8,128)(2,1)S(1)}, s16[1040,512]{1,0:T(8,128)(2,1)S(1)}, u32[]{:S(2)}, u32[]{:S(2)}) collective-permute-start(s16[1040,512]{1,0:T(8,128)(2,1)S(1)} %get-tuple-element.29), channel_id=1, source_target_pairs={{96,0},{98,2},{100,4},{102,6},{104,8},{106,10},{108,12},{110,14},{... | collective-permute-start | bytes 3194888 | tf_op jit(solution)/shard_map/ppermute | solution.py:316
  69.8 3.5 %collective-permute-done.3.one.one_scale = s16[1040,512]{1,0:T(8,128)(2,1)S(1)} collective-permute-done((s16[1040,512]{1,0:T(8,128)(2,1)S(1)}, s16[1040,512]{1,0:T(8,128)(2,1)S(1)}, u32[]{:S(2)}, u32[]{:S(2)}) %collective-permute-start.3) | collective-permute-done | bytes 1064992 | tf_op jit(solution)/shard_map/ppermute | solution.py:316
  73.2 1.3 %collective-permute-start.9 = (bf16[512,1024]{1,0:T(8,128)(2,1)S(1)}, bf16[512,1024]{1,0:T(8,128)(2,1)S(1)}, u32[]{:S(2)}, u32[]{:S(2)}) collective-permute-start(bf16[512,1024]{1,0:T(8,128)(2,1)S(1)} %get-tuple-element.33), channel_id=1, source_target_pairs={{64,96},{66,98},{68,100},{70,102},{72,104},{74,106},{76,108},{78,1... | collective-permute-start | bytes 3145736 | tf_op jit(solution)/shard_map/ppermute | solution.py:316
  74.5 20.1 %collective-permute-done.4.two.two_scale = s16[1040,512]{1,0:T(8,128)(2,1)S(1)} collective-permute-done((s16[1040,512]{1,0:T(8,128)(2,1)S(1)}, s16[1040,512]{1,0:T(8,128)(2,1)S(1)}, u32[]{:S(2)}, u32[]{:S(2)}) %collective-permute-start.4) | collective-permute-done | bytes 1064992 | tf_op jit(solution)/shard_map/ppermute | solution.py:316
  94.6 1.3 %collective-permute-start.8 = (bf16[512,1024]{1,0:T(8,128)(2,1)S(1)}, bf16[512,1024]{1,0:T(8,128)(2,1)S(1)}, u32[]{:S(2)}, u32[]{:S(2)}) collective-permute-start(bf16[512,1024]{1,0:T(8,128)(2,1)S(1)} %get-tuple-element.33), channel_id=1, source_target_pairs={{0,64},{2,66},{4,68},{6,70},{8,72},{10,74},{12,76},{14,78},{16,80}... | collective-permute-start | bytes 3145736 | tf_op jit(solution)/shard_map/ppermute | solution.py:316
  96.0 2.0 %gate.1 = f32[1024,512]{1,0:T(8,128)} custom-call(s32[1024,512]{1,0:T(8,128)S(1)} %copy-done, f32[1024,512]{1,0:T(8,128)S(1)} %get-tuple-element.21.own, s16[1040,512]{1,0:T(8,128)(2,1)S(1)} %collective-permute-done.3.one.one_scale, s16[1040,512]{1,0:T(8,128)(2,1)S(1)} %collective-permute-done.4.two.two_scale, ...), custom_call_target="tpu_custom_call" | custom-call | flops 4194304 | bytes 9437184 | tf_op jit(solution)/shard_map/gate/pallas_call | solution.py:335
  97.9 0.0 collective-permute-done.6.o_come.o_scale
  97.9 0.0 collective-permute-done.9.r_b
  98.0 24.0 %collective-permute-done.8.r_a = bf16[512,1024]{1,0:T(8,128)(2,1)S(1)} collective-permute-done((bf16[512,1024]{1,0:T(8,128)(2,1)S(1)}, bf16[512,1024]{1,0:T(8,128)(2,1)S(1)}, u32[]{:S(2)}, u32[]{:S(2)}) %collective-permute-start.8) | collective-permute-done | bytes 1048608 | tf_op jit(solution)/shard_map/ppermute | solution.py:316
  121.9 0.0 collective-permute-done.7.b_come.b_scale
  121.9 3.7 %weave.1 = bf16[512,4,1024]{2,1,0:T(4,128)(2,1)} custom-call(s32[3]{0:T(128)S(1)} %copy-done.2, f32[512,1024]{1,0:T(8,128)S(1)} %copy-done.1, s16[528,1024]{1,0:T(8,128)(2,1)S(1)} %collective-permute-done.6.o_come.o_scale, s16[528,1024]{1,0:T(8,128)(2,1)S(1)} %collective-permute-done.6.o_come.o_scale, f32[512,1024]{1,0:T(8,128)S(1)} %get-tuple-element.32.b_keep, ...), custom_call_target="tpu_custom_call" | custom-call | flops 1073741824 | bytes 8388608 | tf_op jit(solution)/shard_map/weave/pallas_call | solution.py:299
  (12 shorter events, 0.0 us)
Async XLA Ops:
  1.2 21.8 %copy-start.2 = (s32[3]{0:T(128)S(1)}, s32[3]{0:T(128)}, u32[]{:S(2)}) copy-start(s32[3]{0:T(128)} %pad_add_fusion.idx) | copy-start | bytes 40
  17.8 34.5 %collective-permute-start.1 = (s16[1040,512]{1,0:T(8,128)(2,1)}, s16[1040,512]{1,0:T(8,128)(2,1)S(1)}, u32[]{:S(2)}, u32[]{:S(2)}) collective-permute-start(s16[1040,512]{1,0:T(8,128)(2,1)} %get-tuple-element.19), channel_id=1, source_target_pairs={{0,96},{2,98},{4,100},{6,102},{8,104},{10,106},{12,108},{14,110},{... | collective-permute-start | bytes 3194888 | tf_op jit(solution)/shard_map/ppermute | solution.py:316
  19.1 31.9 %collective-permute-start = (s16[1040,512]{1,0:T(8,128)(2,1)}, s16[1040,512]{1,0:T(8,128)(2,1)S(1)}, u32[]{:S(2)}, u32[]{:S(2)}) collective-permute-start(s16[1040,512]{1,0:T(8,128)(2,1)} %get-tuple-element.19), channel_id=1, source_target_pairs={{0,32},{2,34},{4,36},{6,38},{8,40},{10,42},{12,44},{14,46},{16,48}... | collective-permute-start | bytes 3194888 | tf_op jit(solution)/shard_map/ppermute | solution.py:316
  19.8 33.5 %collective-permute-start.2 = (s16[528,1024]{1,0:T(8,128)(2,1)}, s16[528,1024]{1,0:T(8,128)(2,1)S(1)}, u32[]{:S(2)}, u32[]{:S(2)}) collective-permute-start(s16[528,1024]{1,0:T(8,128)(2,1)} %get-tuple-element.24), channel_id=1, source_target_pairs={{0,1},{1,0},{2,3},{3,2},{4,5},{5,4},{6,7},{7,6},{8,9},{9,8},{10,11... | collective-permute-start | bytes 3244040 | tf_op jit(solution)/shard_map/ppermute | solution.py:320
  23.1 2.2 %copy-start.7 = (bf16[1024,2048]{1,0:T(8,128)(2,1)S(1)}, bf16[1024,2048]{1,0:T(8,128)(2,1)}, u32[]{:S(2)}) copy-start(bf16[1024,2048]{1,0:T(8,128)(2,1)} %get-tuple-element.20.e) | copy-start | bytes 12582916
  42.1 31.1 %collective-permute-start.3 = (s16[1040,512]{1,0:T(8,128)(2,1)S(1)}, s16[1040,512]{1,0:T(8,128)(2,1)S(1)}, u32[]{:S(2)}, u32[]{:S(2)}) collective-permute-start(s16[1040,512]{1,0:T(8,128)(2,1)S(1)} %get-tuple-element.27), channel_id=1, source_target_pairs={{96,64},{98,66},{100,68},{102,70},{104,72},{106,74},{108,76},{110,... | collective-permute-start | bytes 3194888 | tf_op jit(solution)/shard_map/ppermute | solution.py:316
  49.4 45.2 %collective-permute-start.4 = (s16[1040,512]{1,0:T(8,128)(2,1)S(1)}, s16[1040,512]{1,0:T(8,128)(2,1)S(1)}, u32[]{:S(2)}, u32[]{:S(2)}) collective-permute-start(s16[1040,512]{1,0:T(8,128)(2,1)S(1)} %get-tuple-element.28), channel_id=1, source_target_pairs={{96,32},{98,34},{100,36},{102,38},{104,40},{106,42},{108,44},{110,... | collective-permute-start | bytes 3194888 | tf_op jit(solution)/shard_map/ppermute | solution.py:316
  51.0 1.0 copy-start.5
  51.9 46.0 %collective-permute-start.6 = (s16[528,1024]{1,0:T(8,128)(2,1)}, s16[528,1024]{1,0:T(8,128)(2,1)S(1)}, u32[]{:S(2)}, u32[]{:S(2)}) collective-permute-start(s16[528,1024]{1,0:T(8,128)(2,1)} %get-tuple-element.31), channel_id=1, source_target_pairs={{0,1},{1,0},{2,3},{3,2},{4,5},{5,4},{6,7},{7,6},{8,9},{9,8},{10,11... | collective-permute-start | bytes 3244040 | tf_op jit(solution)/shard_map/ppermute | solution.py:320
  52.3 1.0 copy-start.3
  53.3 1.2 copy-start.4
  54.5 1.2 copy-start.6
  55.8 1.6 %copy-start.8 = (f32[512,1024]{1,0:T(8,128)S(1)}, f32[512,1024]{1,0:T(8,128)}, u32[]{:S(2)}) copy-start(f32[512,1024]{1,0:T(8,128)} %get-tuple-element.23.a_keep) | copy-start | bytes 6291460
  57.4 38.6 %copy-start = (s32[1024,512]{1,0:T(8,128)S(1)}, s32[1024,512]{1,0:T(8,128)}, u32[]{:S(2)}) copy-start(s32[1024,512]{1,0:T(8,128)} %mask) | copy-start | bytes 6291460
  65.2 56.8 %collective-permute-start.7 = (s16[528,1024]{1,0:T(8,128)(2,1)S(1)}, s16[528,1024]{1,0:T(8,128)(2,1)S(1)}, u32[]{:S(2)}, u32[]{:S(2)}) collective-permute-start(s16[528,1024]{1,0:T(8,128)(2,1)S(1)} %get-tuple-element.25), channel_id=1, source_target_pairs={{0,1},{1,0},{2,3},{3,2},{4,5},{5,4},{6,7},{7,6},{8,9},{9,8},{10,11... | collective-permute-start | bytes 3244040 | tf_op jit(solution)/shard_map/ppermute | solution.py:320
  68.4 27.5 %collective-permute-start.5 = (s16[1040,512]{1,0:T(8,128)(2,1)S(1)}, s16[1040,512]{1,0:T(8,128)(2,1)S(1)}, u32[]{:S(2)}, u32[]{:S(2)}) collective-permute-start(s16[1040,512]{1,0:T(8,128)(2,1)S(1)} %get-tuple-element.29), channel_id=1, source_target_pairs={{96,0},{98,2},{100,4},{102,6},{104,8},{106,10},{108,12},{110,14},{... | collective-permute-start | bytes 3194888 | tf_op jit(solution)/shard_map/ppermute | solution.py:316
  73.2 24.7 %collective-permute-start.9 = (bf16[512,1024]{1,0:T(8,128)(2,1)S(1)}, bf16[512,1024]{1,0:T(8,128)(2,1)S(1)}, u32[]{:S(2)}, u32[]{:S(2)}) collective-permute-start(bf16[512,1024]{1,0:T(8,128)(2,1)S(1)} %get-tuple-element.33), channel_id=1, source_target_pairs={{64,96},{66,98},{68,100},{70,102},{72,104},{74,106},{76,108},{78,1... | collective-permute-start | bytes 3145736 | tf_op jit(solution)/shard_map/ppermute | solution.py:316
  94.6 27.3 %collective-permute-start.8 = (bf16[512,1024]{1,0:T(8,128)(2,1)S(1)}, bf16[512,1024]{1,0:T(8,128)(2,1)S(1)}, u32[]{:S(2)}, u32[]{:S(2)}) collective-permute-start(bf16[512,1024]{1,0:T(8,128)(2,1)S(1)} %get-tuple-element.33), channel_id=1, source_target_pairs={{0,64},{2,66},{4,68},{6,70},{8,72},{10,74},{12,76},{14,78},{16,80}... | collective-permute-start | bytes 3145736 | tf_op jit(solution)/shard_map/ppermute | solution.py:316
  96.0 26.0 %copy-start.1 = (f32[512,1024]{1,0:T(8,128)S(1)}, f32[512,1024]{1,0:T(8,128)}, u32[]{:S(2)}) copy-start(f32[512,1024]{1,0:T(8,128)} %get-tuple-element.30.o_keep) | copy-start | bytes 6291460
where the time goes:
time: 126 us
  waiting for transfers between devices  47.6 us (38%)
  Pallas kernels  46.8 us (37%)
  starting transfers between devices  21.6 us (17%)
  local copies, waits for them, and re-layouts  8.23 us (7%)
    ppermute x7, waiting for transfers between devices, moved(): lax.ppermute(array, 'dst', [(a * group + i, b * group + i) for a, b in pa...  47.6 us
    pallas_call x1, Pallas kernels, partials(): pl.pallas_call(partial_kernel, name='partials', grid_spec=pltpu.PrefetchS...  16.8 us
    pallas_call x1, Pallas kernels, first_terms(): pl.pallas_call(first_kernel, name='first_terms', grid_spec=pltpu.Prefetch...  16.5 us
    ppermute x7, starting transfers between devices, moved(): lax.ppermute(array, 'dst', [(a * group + i, b * group + i) for a, b in pa...  14.8 us
    unnamed x18, local copies, waits for them, and re-layouts  8.23 us
    pallas_call x1, Pallas kernels, more_terms(): pl.pallas_call(more_kernel, name='more_terms', grid_spec=pltpu.PrefetchSc...  7.79 us
    ppermute x3, starting transfers between devices, swapped(): return lax.ppermute(array, 'tok', [(0, 1), (1, 0)])  6.87 us
    pallas_call x1, Pallas kernels, weave(): pl.pallas_call(weave_kernel, name='weave', grid_spec=pltpu.PrefetchScalar...  3.69 us
  transfers between devices with their start and end apart: 10, of which 3 were waited for; matrix products, arithmetic and copies ran while one was open for 0% of the time, Pallas kernels for 21%

commit v1 on v0

--- a/solution.py
+++ b/solution.py
@@ -59,7 +59,7 @@
 SUB = 64
 
 
-def first_kernel(idx, er, lat, own_e, l_code, a_code, a_keep, o_code, o_keep, pick, e_a, a_send, o_send):
+def first_kernel(idx, er, lat, own_e, l_code, a_code, a_keep, o_code, pick, e_a, a_send, o_send):
     step = pl.program_id(0)
     tokens, _, width = er.shape
     half = width // 2
@@ -85,7 +85,6 @@
         out[...] = term + jnp.where(step > 0, out[...], 0.0)
 
     add(o_send, own_e, send_at)
-    add(o_keep, own_e, keep_at)
 
     @pl.when(early)
     def _():
@@ -129,7 +128,6 @@
                 whole_code,
                 whole,
                 whole_code,
-                whole,
             ],
             scratch_shapes=[
                 pltpu.VMEM((2 * SUB, LAYERS * SUB), BF),
@@ -144,78 +142,123 @@
             code,
             shape,
             code,
-            shape,
         ],
-        compiler_params=params(),
+        compiler_params=params(38),
         cost_estimate=cost(16 * tokens * f * width, 30 << 20),
     )(idx, errors, latents)
 
 
-def more_kernel(idx, near, far, e, a_keep, a_come, a_scale, a_done, code, keep, left):
-    step = pl.program_id(0)
+def more_kernel(idx, near, far, e, code, left):
     rows = near.shape[0] - SCALE_ROWS
     late = idx[0] > 0
-    a_done[...] = (a_keep[...] + wide(a_come[...]) * unit(a_scale[...])).astype(BF)
-
-    @pl.when((step == 0) & late)
+
+    @pl.when((pl.program_id(0) == 0) & late)
     def _():
         both = near[...].astype(jnp.int32) + far[...].astype(jnp.int32)
         left[...] = split_transposed(both[:rows].astype(F32) * jnp.exp2(both[rows : rows + 1].astype(F32) - 15))
 
-    def term():
+    @pl.when(late)
+    def _():
         right = e[...]
-        return jnp.dot(left[...], jnp.concatenate([right, right], axis=0), preferred_element_type=F32)
-
-    @pl.when((step < 2) & late)
-    def _():
-        encode(term(), code)
-
-    @pl.when((step >= 2) & late)
-    def _():
-        keep[...] = term()
-
-
-def more_terms(idx, near, far, e, a_keep, a_come):
+        encode(jnp.dot(left[...], jnp.concatenate([right, right], axis=0), preferred_element_type=F32), code)
+
+
+def more_terms(idx, near, far, e):
     rows, f = near.shape
     tokens, width = e.shape
     tile = width // 4
     half = width // 2
-    part = pl.BlockSpec((f // 4, half), lambda i, s: (i, 0))
     return pl.pallas_call(
         more_kernel,
         name="more_terms",
         grid_spec=pltpu.PrefetchScalarGridSpec(
             num_scalar_prefetch=1,
-            grid=(4,),
+            grid=(2,),
             in_specs=[
                 pl.BlockSpec((rows, f), lambda i, s: (0, 0)),
                 pl.BlockSpec((rows, f), lambda i, s: (0, 0)),
-                pl.BlockSpec((tokens, tile), lambda i, s: (0, lax.rem(i + 2 * (1 - s[2]), 4))),
-                part,
-                part,
-                pl.BlockSpec((SCALE_ROWS, half), lambda i, s: (f // SCALE_ROWS, 0)),
+                pl.BlockSpec((tokens, tile), lambda i, s: (0, i + 2 * (1 - s[2]))),
             ],
             out_specs=[
-                part,
-                pl.BlockSpec((f + SCALE_ROWS, tile), lambda i, s: (0, jnp.minimum(i, 1))),
-                pl.BlockSpec((f, tile), lambda i, s: (0, jnp.maximum(i - 2, 0))),
-            ],
+                pl.BlockSpec((f + SCALE_ROWS, tile), lambda i, s: (0, i)),
+                pl.BlockSpec((f, 2 * tokens), lambda i, s: (0, 0)),
+            ],
+        ),
+        out_shape=[
+            jax.ShapeDtypeStruct((f + SCALE_ROWS, half), I16),
+            jax.ShapeDtypeStruct((f, 2 * tokens), BF),
+        ],
+        compiler_params=params(26),
+        cost_estimate=cost(2 * tokens * f * width, 8 << 20),
+    )(idx, near, far, e)
+
+
+def rest_kernel(idx, lat, b_left, e, w0, o_keep, b_keep, own, o_left):
+    step = pl.program_id(0)
+    _, tile = o_keep.shape
+    half = e.shape[1] // 2
+
+    @pl.when(step == 0)
+    def _():
+        o_left[...] = split_transposed(lat[...])
+
+    right = e[:, pl.ds(pl.multiple_of(idx[2] * half + step * tile, tile), tile)]
+    right = jnp.concatenate([right, right], axis=0)
+    o_keep[...] = jnp.dot(o_left[...], right, preferred_element_type=F32)
+    b_keep[...] = jnp.dot(b_left[...], right, preferred_element_type=F32)
+    own[...] = lax.dot_general(e[...], w0[...], (((1,), (1,)), ((), ())), preferred_element_type=F32)
+
+
+def rest_terms(idx, latents, b_left, e, w0):
+    tokens, f = latents.shape
+    width = e.shape[1]
+    half = width // 2
+    kept = pl.BlockSpec((f, half // 2), lambda i, s: (0, i))
+    return pl.pallas_call(
+        rest_kernel,
+        name="rest_terms",
+        grid_spec=pltpu.PrefetchScalarGridSpec(
+            num_scalar_prefetch=1,
+            grid=(2,),
+            in_specs=[
+                pl.BlockSpec((tokens, f), lambda i, s: (0, 0)),
+                pl.BlockSpec((f, 2 * tokens), lambda i, s: (0, 0)),
+                pl.BlockSpec((tokens, width), lambda i, s: (0, 0)),
+                pl.BlockSpec((f // 2, width), lambda i, s: (i, 0)),
+            ],
+            out_specs=[kept, kept, pl.BlockSpec((tokens, f // 2), lambda i, s: (0, i))],
             scratch_shapes=[pltpu.VMEM((f, 2 * tokens), BF)],
         ),
-        out_shape=[
-            jax.ShapeDtypeStruct((f, half), BF),
-            jax.ShapeDtypeStruct((f + SCALE_ROWS, half), I16),
-            jax.ShapeDtypeStruct((f, half), F32),
-        ],
+        out_shape=[jax.ShapeDtypeStruct((f, half), F32)] * 2 + [jax.ShapeDtypeStruct((tokens, f), F32)],
         compiler_params=params(40),
-        cost_estimate=cost(4 * tokens * f * width, 12 << 20),
-    )(idx, near, far, e, a_keep, a_come, a_come)
+        cost_estimate=cost(6 * tokens * f * width, 16 << 20),
+    )(idx, latents, b_left, e, w0)
+
+
+def join_kernel(keep, come, scale, out):
+    out[...] = (keep[...] + wide(come[...]) * unit(scale[...])).astype(BF)
+
+
+def joined(keep, come):
+    f, width = keep.shape
+    tile = 256
+    block = pl.BlockSpec((tile, width), lambda i: (i, 0))
+    return pl.pallas_call(
+        join_kernel,
+        name="join",
+        grid=(f // tile,),
+        in_specs=[block, block, pl.BlockSpec((SCALE_ROWS, width), lambda i: (f // SCALE_ROWS, 0))],
+        out_specs=block,
+        out_shape=jax.ShapeDtypeStruct((f, width), BF),
+        compiler_params=params(24),
+        cost_estimate=cost(4 * f * width, 4 << 20),
+    )(keep, come, come)
 
 
 W_SUB = 64
 
 
-def partial_kernel(idx, e, w, own, one, two, three, pick, plain):
+def partial_kernel(idx, e, w, zero, one, two, three, pick, plain):
     f, _, width = w.shape
 
     @pl.when(pl.program_id(0) == 0)
@@ -225,24 +268,24 @@
     for j in range(f // W_SUB):
         rows = w[j * W_SUB : (j + 1) * W_SUB].reshape(LAYERS * W_SUB, width)
         got = jnp.dot(pick[...], rows, preferred_element_type=F32).astype(BF)
-        for k in range(LAYERS):
-            plain[k * f + j * W_SUB : k * f + (j + 1) * W_SUB] = got[k * W_SUB : (k + 1) * W_SUB]
-
-    for place in range(LAYERS):
+        zero[j * W_SUB : (j + 1) * W_SUB] = got[:W_SUB]
+        for k in range(1, LAYERS):
+            plain[(k - 1) * f + j * W_SUB : (k - 1) * f + (j + 1) * W_SUB] = got[k * W_SUB : (k + 1) * W_SUB]
+
+    for place in range(1, LAYERS):
 
         @pl.when(idx[0] == place)
         def _():
-            rows = plain[: (place + 1) * f]
+            rows = plain[: place * f]
             terms = lax.dot_general(e[...], rows, (((1,), (1,)), ((), ())), preferred_element_type=F32)
-            own[...] = terms[:, :f]
-            for k, code in ((1, one), (2, two), (3, three))[:place]:
+            for k, code in enumerate((one, two, three)[:place]):
                 encode(terms[:, k * f : (k + 1) * f], code)
 
 
 def partials(idx, e, decoder):
     tokens, width = e.shape
     f = decoder.shape[0]
-    tile = 128
+    tile = 256
     code = pl.BlockSpec((tokens + SCALE_ROWS, tile), lambda i, s: (0, i))
     return pl.pallas_call(
         partial_kernel,
@@ -254,13 +297,13 @@
                 pl.BlockSpec((tokens, width), lambda i, s: (0, 0)),
                 pl.BlockSpec((tile, LAYERS, width), lambda i, s: (i, 0, 0)),
             ],
-            out_specs=[pl.BlockSpec((tokens, tile), lambda i, s: (0, i)), code, code, code],
+            out_specs=[pl.BlockSpec((tile, width), lambda i, s: (i, 0)), code, code, code],
             scratch_shapes=[
                 pltpu.VMEM((LAYERS * W_SUB, LAYERS * W_SUB), BF),
-                pltpu.VMEM((LAYERS * tile, width), BF),
+                pltpu.VMEM(((LAYERS - 1) * tile, width), BF),
             ],
         ),
-        out_shape=[jax.ShapeDtypeStruct((tokens, f), F32)] + [jax.ShapeDtypeStruct((tokens + SCALE_ROWS, f), I16)] * 3,
+        out_shape=[jax.ShapeDtypeStruct((f, width), BF)] + [jax.ShapeDtypeStruct((tokens + SCALE_ROWS, f), I16)] * 3,
         compiler_params=params(40),
         cost_estimate=cost(8 * tokens * f * width, 20 << 20),
     )(idx, e, decoder)
@@ -344,34 +387,33 @@
     )(mask, own, *terms, *terms)
 
 
-def after(array, earlier):
-    return lax.optimization_barrier((array, earlier))[0]
-
-
 def per_device(latents, mask, errors, decoder):
     group = lax.axis_size("dst") // LAYERS
     place = lax.axis_index("dst") // group
     other = jnp.where(place == 0, 2, 3)
     idx = jnp.stack([place, other, lax.axis_index("tok")]).astype(jnp.int32)
 
-    own_e, l_code, a_code, a_keep, o_code, o_keep = first_terms(idx, errors, latents)
+    own_e, l_code, a_code, a_keep, o_code = first_terms(idx, errors, latents)
     a_come = swapped(a_code)
     o_come = swapped(o_code)
     near = moved(l_code, group, [(0, 1), (1, 2)])
     far = moved(l_code, group, [(0, 3)])
 
-    own_p, one_p, two_p, three_p = partials(idx, own_e, decoder)
+    w0, one_p, two_p, three_p = partials(idx, own_e, decoder)
     three = moved(three_p, group, [(3, 0)])
     two = moved(two_p, group, [(3, 1), (2, 0)])
     one = moved(one_p, group, [(3, 2), (2, 1), (1, 0)])
 
-    a_done, b_code, b_keep = more_terms(idx, after(near, own_p), far, own_e, a_keep, a_come)
+    a_done = joined(a_keep, a_come)
+    r_b = moved(a_done, group, [(2, 3)])
+    r_a = moved(a_done, group, [(0, 2), (1, 3)])
+
+    b_code, b_left = more_terms(idx, near, far, own_e)
     b_come = swapped(b_code)
-    r_a = moved(a_done, group, [(0, 2), (1, 3)])
-    r_b = moved(a_done, group, [(2, 3)])
-
-    latent_grad = gated(after(mask, b_code), own_p, (one, two, three))
-    decoder_grad = weave(idx, after(o_keep, latent_grad), o_come, b_keep, b_come, r_a, r_b)
+    o_keep, b_keep, own_p = rest_terms(idx, latents, b_left, own_e, w0)
+
+    latent_grad = gated(mask, own_p, (one, two, three))
+    decoder_grad = weave(idx, o_keep, o_come, b_keep, b_come, r_a, r_b)
     return decoder_grad, latent_grad
 
 

time: 126 us -> 116 us (0.921)
  the two profiles are of different devices: /device:TPU:38 before, /device:TPU:6 now
where the time goes in v1:
time: 116 us; the launch traced here: 115 us
  Pallas kernels  46.8 us (40%)
  waiting for transfers between devices  40.8 us (35%)
  starting transfers between devices  20.7 us (18%)
  local copies, waits for them, and re-layouts  6.12 us (5%)
    ppermute x7, waiting for transfers between devices, moved(): lax.ppermute(array, 'dst', [(a * group + i, b * group + i) for a, b in pa...  40.8 us
    pallas_call x1, Pallas kernels, partials(): pl.pallas_call(partial_kernel, name='partials', grid_spec=pltpu.PrefetchS...  14.6 us
    ppermute x7, starting transfers between devices, moved(): lax.ppermute(array, 'dst', [(a * group + i, b * group + i) for a, b in pa...  13.3 us
    pallas_call x1, Pallas kernels, rest_terms(): pl.pallas_call(rest_kernel, name='rest_terms', grid_spec=pltpu.PrefetchSc...  10.8 us
    pallas_call x1, Pallas kernels, first_terms(): pl.pallas_call(first_kernel, name='first_terms', grid_spec=pltpu.Prefetch...  10.2 us
    ppermute x3, starting transfers between devices, swapped(): return lax.ppermute(array, 'tok', [(0, 1), (1, 0)])  7.48 us
    unnamed x16, local copies, waits for them, and re-layouts  6.12 us
    pallas_call x1, Pallas kernels, more_terms(): pl.pallas_call(more_kernel, name='more_terms', grid_spec=pltpu.PrefetchSc...  5.22 us
  transfers between devices with their start and end apart: 10, of which 4 were waited for; matrix products, arithmetic and copies ran while one was open for 0% of the time, Pallas kernels for 28%

profile of v1, /device:TPU:6, one launch (start us, length us, event | category | flops | bytes accessed | tf_op | source)
XLA Modules:
  0.0 115.4 jit_solution(15087986059062876408)
XLA Ops:
  0.6 0.1 pad_add_fusion.idx
  0.7 1.6 %copy-done.1 = f32[1024,512]{1,0:T(8,128)S(1)} copy-done((f32[1024,512]{1,0:T(8,128)S(1)}, f32[1024,512]{1,0:T(8,128)}, u32[]{:S(2)}) %copy-start.1) | copy-done | bytes 2097176
  2.3 10.2 %first_terms.1 = (bf16[1024,2048]{1,0:T(8,128)(2,1)S(1)}, s16[1040,512]{1,0:T(8,128)(2,1)S(1)}, s16[528,1024]{1,0:T(8,128)(2,1)S(1)}, f32[512,1024]{1,0:T(8,128)S(1)}, s16[528,1024]{1,0:T(8,128)(2,1)S(1)}) custom-call(s32[3]{0:T(128)S(1)} %pad_add_fusion.idx, bf16[1024,4,2048]{2,1,0:T(4,128)(2,1)} %er.1, f32[1024,512]{1,0:T(8,128)S(1)} %copy-done.1), custom_call_target="tpu_custom_call" | custom-call | flops 17179869184 | bytes 31457280 | tf_op jit(solution)/shard_map/first_terms/pallas_call | solution.py:115
  12.5 0.0 copy-start.3
  12.5 1.3 %collective-permute-start.1 = (s16[1040,512]{1,0:T(8,128)(2,1)S(1)}, s16[1040,512]{1,0:T(8,128)(2,1)S(1)}, u32[]{:S(2)}, u32[]{:S(2)}) collective-permute-start(s16[1040,512]{1,0:T(8,128)(2,1)S(1)} %get-tuple-element.16), channel_id=1, source_target_pairs={{0,96},{2,98},{4,100},{6,102},{8,104},{10,106},{12,108},{14,110},{... | collective-permute-start | bytes 3194888 | tf_op jit(solution)/shard_map/ppermute | solution.py:359
  13.8 0.7 collective-permute-start
  14.6 3.5 %collective-permute-start.4 = (s16[528,1024]{1,0:T(8,128)(2,1)S(1)}, s16[528,1024]{1,0:T(8,128)(2,1)S(1)}, u32[]{:S(2)}, u32[]{:S(2)}) collective-permute-start(s16[528,1024]{1,0:T(8,128)(2,1)S(1)} %get-tuple-element.25), channel_id=1, source_target_pairs={{0,1},{1,0},{2,3},{3,2},{4,5},{5,4},{6,7},{7,6},{8,9},{9,8},{10,11... | collective-permute-start | bytes 3244040 | tf_op jit(solution)/shard_map/ppermute | solution.py:363
  18.0 14.6 %partials.1 = (bf16[512,2048]{1,0:T(8,128)(2,1)S(1)}, s16[1040,512]{1,0:T(8,128)(2,1)S(1)}, s16[1040,512]{1,0:T(8,128)(2,1)S(1)}, s16[1040,512]{1,0:T(8,128)(2,1)}) custom-call(s32[3]{0:T(128)S(1)} %pad_add_fusion.idx, bf16[1024,2048]{1,0:T(8,128)(2,1)S(1)} %get-tuple-element.17.e, bf16[512,4,2048]{2,1,0:T(4,128)(2,1)} %w.1), custom_call_target="tpu_custom_call" | custom-call | flops 8589934592 | bytes 20971520 | tf_op jit(solution)/shard_map/partials/pallas_call | solution.py:290
  32.6 1.3 %copy-done.6 = bf16[512,2048]{1,0:T(8,128)(2,1)} copy-done((bf16[512,2048]{1,0:T(8,128)(2,1)}, bf16[512,2048]{1,0:T(8,128)(2,1)S(1)}, u32[]{:S(2)}) %copy-start.6) | copy-done | bytes 2097176
  33.9 5.2 %collective-permute-start.7 = (s16[1040,512]{1,0:T(8,128)(2,1)S(1)}, s16[1040,512]{1,0:T(8,128)(2,1)S(1)}, u32[]{:S(2)}, u32[]{:S(2)}) collective-permute-start(s16[1040,512]{1,0:T(8,128)(2,1)S(1)} %get-tuple-element.27), channel_id=1, source_target_pairs={{96,64},{98,66},{100,68},{102,70},{104,72},{106,74},{108,76},{110,... | collective-permute-start | bytes 3194888 | tf_op jit(solution)/shard_map/ppermute | solution.py:359
  39.2 1.8 %collective-permute-start.8 = (s16[1040,512]{1,0:T(8,128)(2,1)S(1)}, s16[1040,512]{1,0:T(8,128)(2,1)S(1)}, u32[]{:S(2)}, u32[]{:S(2)}) collective-permute-start(s16[1040,512]{1,0:T(8,128)(2,1)S(1)} %get-tuple-element.28), channel_id=1, source_target_pairs={{96,32},{98,34},{100,36},{102,38},{104,40},{106,42},{108,44},{110,... | collective-permute-start | bytes 3194888 | tf_op jit(solution)/shard_map/ppermute | solution.py:359
  41.0 1.5 %collective-permute-done.1.far = s16[1040,512]{1,0:T(8,128)(2,1)S(1)} collective-permute-done((s16[1040,512]{1,0:T(8,128)(2,1)S(1)}, s16[1040,512]{1,0:T(8,128)(2,1)S(1)}, u32[]{:S(2)}, u32[]{:S(2)}) %collective-permute-start.1) | collective-permute-done | bytes 1064992 | tf_op jit(solution)/shard_map/ppermute | solution.py:359
  42.4 4.0 %collective-permute-start.2 = (s16[528,1024]{1,0:T(8,128)(2,1)S(1)}, s16[528,1024]{1,0:T(8,128)(2,1)S(1)}, u32[]{:S(2)}, u32[]{:S(2)}) collective-permute-start(s16[528,1024]{1,0:T(8,128)(2,1)S(1)} %get-tuple-element.21), channel_id=1, source_target_pairs={{0,1},{1,0},{2,3},{3,2},{4,5},{5,4},{6,7},{7,6},{8,9},{9,8},{10,11... | collective-permute-start | bytes 3244040 | tf_op jit(solution)/shard_map/ppermute | solution.py:363
  46.5 0.0 collective-permute-done.near
  46.5 5.2 %more_terms.1 = (s16[528,1024]{1,0:T(8,128)(2,1)}, bf16[512,2048]{1,0:T(8,128)(2,1)S(1)}) custom-call(s32[3]{0:T(128)S(1)} %pad_add_fusion.idx, s16[1040,512]{1,0:T(8,128)(2,1)S(1)} %collective-permute-done.near, s16[1040,512]{1,0:T(8,128)(2,1)S(1)} %collective-permute-done.1.far, bf16[1024,2048]{1,0:T(8,128)(2,1)S(1)} %get-tuple-element.17.e), custom_call_target="tpu_custom_call" | custom-call | flops 2147483648 | bytes 8388608 | tf_op jit(solution)/shard_map/more_terms/pallas_call | solution.py:171
  51.7 0.0 collective-permute-start.3
  51.7 0.0 collective-permute-done.4.come.scale
  51.7 1.4 %collective-permute-start.9 = (s16[1040,512]{1,0:T(8,128)(2,1)}, s16[1040,512]{1,0:T(8,128)(2,1)S(1)}, u32[]{:S(2)}, u32[]{:S(2)}) collective-permute-start(s16[1040,512]{1,0:T(8,128)(2,1)} %get-tuple-element.29), channel_id=1, source_target_pairs={{96,0},{98,2},{100,4},{102,6},{104,8},{106,10},{108,12},{110,14},{... | collective-permute-start | bytes 3194888 | tf_op jit(solution)/shard_map/ppermute | solution.py:359
  53.1 0.0 copy-start.2
  53.2 0.4 join.1
  53.5 9.4 %collective-permute-done.7.one.one_scale = s16[1040,512]{1,0:T(8,128)(2,1)S(1)} collective-permute-done((s16[1040,512]{1,0:T(8,128)(2,1)S(1)}, s16[1040,512]{1,0:T(8,128)(2,1)S(1)}, u32[]{:S(2)}, u32[]{:S(2)}) %collective-permute-start.7) | collective-permute-done | bytes 1064992 | tf_op jit(solution)/shard_map/ppermute | solution.py:359
  63.0 1.3 %collective-permute-start.6 = (bf16[512,1024]{1,0:T(8,128)(2,1)S(1)}, bf16[512,1024]{1,0:T(8,128)(2,1)S(1)}, u32[]{:S(2)}, u32[]{:S(2)}) collective-permute-start(bf16[512,1024]{1,0:T(8,128)(2,1)S(1)} %join.1), channel_id=1, source_target_pairs={{64,96},{66,98},{68,100},{70,102},{72,104},{74,106},{76,108},{78,1... | collective-permute-start | bytes 3145736 | tf_op jit(solution)/shard_map/ppermute | solution.py:359
  64.3 20.1 %collective-permute-done.8.two.two_scale = s16[1040,512]{1,0:T(8,128)(2,1)S(1)} collective-permute-done((s16[1040,512]{1,0:T(8,128)(2,1)S(1)}, s16[1040,512]{1,0:T(8,128)(2,1)S(1)}, u32[]{:S(2)}, u32[]{:S(2)}) %collective-permute-start.8) | collective-permute-done | bytes 1064992 | tf_op jit(solution)/shard_map/ppermute | solution.py:359
  84.4 1.5 %collective-permute-start.5 = (bf16[512,1024]{1,0:T(8,128)(2,1)S(1)}, bf16[512,1024]{1,0:T(8,128)(2,1)S(1)}, u32[]{:S(2)}, u32[]{:S(2)}) collective-permute-start(bf16[512,1024]{1,0:T(8,128)(2,1)S(1)} %join.1), channel_id=1, source_target_pairs={{0,64},{2,66},{4,68},{6,70},{8,72},{10,74},{12,76},{14,78},{16,80}... | collective-permute-start | bytes 3145736 | tf_op jit(solution)/shard_map/ppermute | solution.py:359
  85.9 0.0 copy-start.5
  85.9 1.6 %copy-done.5 = bf16[512,2048]{1,0:T(8,128)(2,1)S(1)} copy-done((bf16[512,2048]{1,0:T(8,128)(2,1)S(1)}, bf16[512,2048]{1,0:T(8,128)(2,1)}, u32[]{:S(2)}) %copy-start.5) | copy-done | bytes 2097176
  87.5 1.6 %copy-done.7 = bf16[512,2048]{1,0:T(8,128)(2,1)S(1)} copy-done((bf16[512,2048]{1,0:T(8,128)(2,1)S(1)}, bf16[512,2048]{1,0:T(8,128)(2,1)}, u32[]{:S(2)}) %copy-start.7) | copy-done | bytes 2097176
  89.1 10.8 %rest_terms.1 = (f32[512,1024]{1,0:T(8,128)S(1)}, f32[512,1024]{1,0:T(8,128)S(1)}, f32[1024,512]{1,0:T(8,128)S(1)}) custom-call(s32[3]{0:T(128)S(1)} %pad_add_fusion.idx, f32[1024,512]{1,0:T(8,128)S(1)} %copy-done.2, bf16[512,2048]{1,0:T(8,128)(2,1)S(1)} %copy-done.5, bf16[1024,2048]{1,0:T(8,128)(2,1)} %copy-done.3, bf16[512,2048]{1,0:T(8,128)(2,1)S(1)} %copy-done.7), custom_call_target="tpu_custom_call" | custom-call | flops 6442450944 | bytes 16777216 | tf_op jit(solution)/shard_map/rest_terms/pallas_call | solution.py:217
  99.9 2.0 %gate.1 = f32[1024,512]{1,0:T(8,128)} custom-call(s32[1024,512]{1,0:T(8,128)S(1)} %copy-done, f32[1024,512]{1,0:T(8,128)S(1)} %get-tuple-element.26.own, s16[1040,512]{1,0:T(8,128)(2,1)S(1)} %collective-permute-done.7.one.one_scale, s16[1040,512]{1,0:T(8,128)(2,1)S(1)} %collective-permute-done.8.two.two_scale, ...), custom_call_target="tpu_custom_call" | custom-call | flops 4194304 | bytes 9437184 | tf_op jit(solution)/shard_map/gate/pallas_call | solution.py:378
  101.9 0.0 collective-permute-done.6.r_b
  101.9 9.8 %collective-permute-done.5.r_a = bf16[512,1024]{1,0:T(8,128)(2,1)S(1)} collective-permute-done((bf16[512,1024]{1,0:T(8,128)(2,1)S(1)}, bf16[512,1024]{1,0:T(8,128)(2,1)S(1)}, u32[]{:S(2)}, u32[]{:S(2)}) %collective-permute-start.5) | collective-permute-done | bytes 1048608 | tf_op jit(solution)/shard_map/ppermute | solution.py:359
  111.7 3.7 %weave.1 = bf16[512,4,1024]{2,1,0:T(4,128)(2,1)} custom-call(s32[3]{0:T(128)S(1)} %pad_add_fusion.idx, f32[512,1024]{1,0:T(8,128)S(1)} %get-tuple-element.20.o_keep, s16[528,1024]{1,0:T(8,128)(2,1)S(1)} %collective-permute-done.2.o_come.o_scale, s16[528,1024]{1,0:T(8,128)(2,1)S(1)} %collective-permute-done.2.o_come.o_scale, ...), custom_call_target="tpu_custom_call" | custom-call | flops 1073741824 | bytes 8388608 | tf_op jit(solution)/shard_map/weave/pallas_call | solution.py:342
  (12 shorter events, 0.0 us)
Async XLA Ops:
  0.7 1.6 %copy-start.1 = (f32[1024,512]{1,0:T(8,128)S(1)}, f32[1024,512]{1,0:T(8,128)}, u32[]{:S(2)}) copy-start(f32[1024,512]{1,0:T(8,128)} %lat.3) | copy-start | bytes 6291460
  12.5 33.9 %copy-start.3 = (bf16[1024,2048]{1,0:T(8,128)(2,1)}, bf16[1024,2048]{1,0:T(8,128)(2,1)S(1)}, u32[]{:S(2)}) copy-start(bf16[1024,2048]{1,0:T(8,128)(2,1)S(1)} %get-tuple-element.17.e) | copy-start | bytes 12582916
  12.5 29.9 %collective-permute-start.1 = (s16[1040,512]{1,0:T(8,128)(2,1)S(1)}, s16[1040,512]{1,0:T(8,128)(2,1)S(1)}, u32[]{:S(2)}, u32[]{:S(2)}) collective-permute-start(s16[1040,512]{1,0:T(8,128)(2,1)S(1)} %get-tuple-element.16), channel_id=1, source_target_pairs={{0,96},{2,98},{4,100},{6,102},{8,104},{10,106},{12,108},{14,110},{... | collective-permute-start | bytes 3194888 | tf_op jit(solution)/shard_map/ppermute | solution.py:359
  13.8 32.6 %collective-permute-start = (s16[1040,512]{1,0:T(8,128)(2,1)S(1)}, s16[1040,512]{1,0:T(8,128)(2,1)S(1)}, u32[]{:S(2)}, u32[]{:S(2)}) collective-permute-start(s16[1040,512]{1,0:T(8,128)(2,1)S(1)} %get-tuple-element.16), channel_id=1, source_target_pairs={{0,32},{2,34},{4,36},{6,38},{8,40},{10,42},{12,44},{14,46},{16,48}... | collective-permute-start | bytes 3194888 | tf_op jit(solution)/shard_map/ppermute | solution.py:359
  14.6 37.1 %collective-permute-start.4 = (s16[528,1024]{1,0:T(8,128)(2,1)S(1)}, s16[528,1024]{1,0:T(8,128)(2,1)S(1)}, u32[]{:S(2)}, u32[]{:S(2)}) collective-permute-start(s16[528,1024]{1,0:T(8,128)(2,1)S(1)} %get-tuple-element.25), channel_id=1, source_target_pairs={{0,1},{1,0},{2,3},{3,2},{4,5},{5,4},{6,7},{7,6},{8,9},{9,8},{10,11... | collective-permute-start | bytes 3244040 | tf_op jit(solution)/shard_map/ppermute | solution.py:363
  32.6 1.3 %copy-start.6 = (bf16[512,2048]{1,0:T(8,128)(2,1)}, bf16[512,2048]{1,0:T(8,128)(2,1)S(1)}, u32[]{:S(2)}) copy-start(bf16[512,2048]{1,0:T(8,128)(2,1)S(1)} %get-tuple-element.19.w0) | copy-start | bytes 6291460
  33.9 29.0 %collective-permute-start.7 = (s16[1040,512]{1,0:T(8,128)(2,1)S(1)}, s16[1040,512]{1,0:T(8,128)(2,1)S(1)}, u32[]{:S(2)}, u32[]{:S(2)}) collective-permute-start(s16[1040,512]{1,0:T(8,128)(2,1)S(1)} %get-tuple-element.27), channel_id=1, source_target_pairs={{96,64},{98,66},{100,68},{102,70},{104,72},{106,74},{108,76},{110,... | collective-permute-start | bytes 3194888 | tf_op jit(solution)/shard_map/ppermute | solution.py:359
  39.2 45.2 %collective-permute-start.8 = (s16[1040,512]{1,0:T(8,128)(2,1)S(1)}, s16[1040,512]{1,0:T(8,128)(2,1)S(1)}, u32[]{:S(2)}, u32[]{:S(2)}) collective-permute-start(s16[1040,512]{1,0:T(8,128)(2,1)S(1)} %get-tuple-element.28), channel_id=1, source_target_pairs={{96,32},{98,34},{100,36},{102,38},{104,40},{106,42},{108,44},{110,... | collective-permute-start | bytes 3194888 | tf_op jit(solution)/shard_map/ppermute | solution.py:359
  42.4 59.4 %collective-permute-start.2 = (s16[528,1024]{1,0:T(8,128)(2,1)S(1)}, s16[528,1024]{1,0:T(8,128)(2,1)S(1)}, u32[]{:S(2)}, u32[]{:S(2)}) collective-permute-start(s16[528,1024]{1,0:T(8,128)(2,1)S(1)} %get-tuple-element.21), channel_id=1, source_target_pairs={{0,1},{1,0},{2,3},{3,2},{4,5},{5,4},{6,7},{7,6},{8,9},{9,8},{10,11... | collective-permute-start | bytes 3244040 | tf_op jit(solution)/shard_map/ppermute | solution.py:363
  51.7 1.9 %copy-start.4 = (bf16[512,2048]{1,0:T(8,128)(2,1)}, bf16[512,2048]{1,0:T(8,128)(2,1)S(1)}, u32[]{:S(2)}) copy-start(bf16[512,2048]{1,0:T(8,128)(2,1)S(1)} %get-tuple-element.18.b_left) | copy-start | bytes 6291460
  51.7 60.0 %collective-permute-start.3 = (s16[528,1024]{1,0:T(8,128)(2,1)}, s16[528,1024]{1,0:T(8,128)(2,1)S(1)}, u32[]{:S(2)}, u32[]{:S(2)}) collective-permute-start(s16[528,1024]{1,0:T(8,128)(2,1)} %get-tuple-element.23), channel_id=1, source_target_pairs={{0,1},{1,0},{2,3},{3,2},{4,5},{5,4},{6,7},{7,6},{8,9},{9,8},{10,11... | collective-permute-start | bytes 3244040 | tf_op jit(solution)/shard_map/ppermute | solution.py:363
  51.7 48.2 %collective-permute-start.9 = (s16[1040,512]{1,0:T(8,128)(2,1)}, s16[1040,512]{1,0:T(8,128)(2,1)S(1)}, u32[]{:S(2)}, u32[]{:S(2)}) collective-permute-start(s16[1040,512]{1,0:T(8,128)(2,1)} %get-tuple-element.29), channel_id=1, source_target_pairs={{96,0},{98,2},{100,4},{102,6},{104,8},{106,10},{108,12},{110,14},{... | collective-permute-start | bytes 3194888 | tf_op jit(solution)/shard_map/ppermute | solution.py:359
  53.1 32.8 %copy-start.2 = (f32[1024,512]{1,0:T(8,128)S(1)}, f32[1024,512]{1,0:T(8,128)}, u32[]{:S(2)}) copy-start(f32[1024,512]{1,0:T(8,128)} %lat.3) | copy-start | bytes 6291460
  63.0 38.9 %collective-permute-start.6 = (bf16[512,1024]{1,0:T(8,128)(2,1)S(1)}, bf16[512,1024]{1,0:T(8,128)(2,1)S(1)}, u32[]{:S(2)}, u32[]{:S(2)}) collective-permute-start(bf16[512,1024]{1,0:T(8,128)(2,1)S(1)} %join.1), channel_id=1, source_target_pairs={{64,96},{66,98},{68,100},{70,102},{72,104},{74,106},{76,108},{78,1... | collective-permute-start | bytes 3145736 | tf_op jit(solution)/shard_map/ppermute | solution.py:359
  84.4 27.3 %collective-permute-start.5 = (bf16[512,1024]{1,0:T(8,128)(2,1)S(1)}, bf16[512,1024]{1,0:T(8,128)(2,1)S(1)}, u32[]{:S(2)}, u32[]{:S(2)}) collective-permute-start(bf16[512,1024]{1,0:T(8,128)(2,1)S(1)} %join.1), channel_id=1, source_target_pairs={{0,64},{2,66},{4,68},{6,70},{8,72},{10,74},{12,76},{14,78},{16,80}... | collective-permute-start | bytes 3145736 | tf_op jit(solution)/shard_map/ppermute | solution.py:359
  85.9 1.6 %copy-start.5 = (bf16[512,2048]{1,0:T(8,128)(2,1)S(1)}, bf16[512,2048]{1,0:T(8,128)(2,1)}, u32[]{:S(2)}) copy-start(bf16[512,2048]{1,0:T(8,128)(2,1)} %copy-done.4) | copy-start | bytes 6291460
  87.5 1.6 %copy-start.7 = (bf16[512,2048]{1,0:T(8,128)(2,1)S(1)}, bf16[512,2048]{1,0:T(8,128)(2,1)}, u32[]{:S(2)}) copy-start(bf16[512,2048]{1,0:T(8,128)(2,1)} %copy-done.6) | copy-start | bytes 6291460
  89.1 10.8 %copy-start = (s32[1024,512]{1,0:T(8,128)S(1)}, s32[1024,512]{1,0:T(8,128)}, u32[]{:S(2)}) copy-start(s32[1024,512]{1,0:T(8,128)} %mask.1) | copy-start | bytes 6291460

commit v2 on v1

--- a/solution.py
+++ b/solution.py
@@ -10,7 +10,7 @@
 BF = jnp.bfloat16
 F32 = jnp.float32
 I16 = jnp.int16
-SCALE_ROWS = 16
+SCALE_ROWS = 8
 
 
 def params(mib=60):
@@ -59,7 +59,7 @@
 SUB = 64
 
 
-def first_kernel(idx, er, lat, own_e, l_code, a_code, a_keep, o_code, pick, e_a, a_send, o_send):
+def first_kernel(idx, er, lat, own_e, e_keep, high, low, l_code, a_code, o_code, pick, e_a, a_send, o_send):
     step = pl.program_id(0)
     tokens, _, width = er.shape
     half = width // 2
@@ -76,6 +76,8 @@
         own_e[j * SUB : (j + 1) * SUB] = got[:SUB]
         e_a[j * SUB : (j + 1) * SUB] = got[SUB:]
     left = split_transposed(lat[pl.ds(pl.multiple_of(step * tokens, tokens), tokens)])
+    high[...] = left[:, :tokens]
+    low[...] = left[:, tokens:]
     keep_at = pl.multiple_of(idx[2] * half, half)
     send_at = pl.multiple_of((1 - idx[2]) * half, half)
 
@@ -89,7 +91,7 @@
     @pl.when(early)
     def _():
         add(a_send, e_a, send_at)
-        add(a_keep, e_a, keep_at)
+        e_keep[...] = e_a[:, pl.ds(keep_at, half)]
 
     @pl.when(last & early)
     def _():
@@ -108,9 +110,9 @@
     tokens, _, width = errors.shape
     f = latents.shape[1]
     half = width // 2
-    whole = pl.BlockSpec((f, half), lambda i, s: (0, 0))
+    left = pl.BlockSpec((f, tile), lambda i, s: (0, i))
     whole_code = pl.BlockSpec((f + SCALE_ROWS, half), lambda i, s: (0, 0))
-    shape = jax.ShapeDtypeStruct((f, half), F32)
+    shape = pltpu.HBM((f, tokens), BF)
     code = jax.ShapeDtypeStruct((f + SCALE_ROWS, half), I16)
     return pl.pallas_call(
         first_kernel,
@@ -124,9 +126,11 @@
             ],
             out_specs=[
                 pl.BlockSpec((tile, width), lambda i, s: (i, 0)),
+                pl.BlockSpec((tile, half), lambda i, s: (i, 0)),
+                left,
+                left,
                 pl.BlockSpec((tokens + SCALE_ROWS, f), lambda i, s: (0, 0)),
                 whole_code,
-                whole,
                 whole_code,
             ],
             scratch_shapes=[
@@ -138,9 +142,11 @@
         ),
         out_shape=[
             jax.ShapeDtypeStruct((tokens, width), BF),
+            pltpu.HBM((tokens, half), BF),
+            shape,
+            shape,
             jax.ShapeDtypeStruct((tokens + SCALE_ROWS, f), I16),
             code,
-            shape,
             code,
         ],
         compiler_params=params(38),
@@ -193,26 +199,23 @@
     )(idx, near, far, e)
 
 
-def rest_kernel(idx, lat, b_left, e, w0, o_keep, b_keep, own, o_left):
+def rest_kernel(idx, high, low, b_left, e, w0, o_keep, b_keep, own):
     step = pl.program_id(0)
     _, tile = o_keep.shape
     half = e.shape[1] // 2
 
-    @pl.when(step == 0)
-    def _():
-        o_left[...] = split_transposed(lat[...])
-
     right = e[:, pl.ds(pl.multiple_of(idx[2] * half + step * tile, tile), tile)]
+    o_keep[...] = jnp.dot(high[...], right, preferred_element_type=F32) + jnp.dot(low[...], right, preferred_element_type=F32)
     right = jnp.concatenate([right, right], axis=0)
-    o_keep[...] = jnp.dot(o_left[...], right, preferred_element_type=F32)
     b_keep[...] = jnp.dot(b_left[...], right, preferred_element_type=F32)
     own[...] = lax.dot_general(e[...], w0[...], (((1,), (1,)), ((), ())), preferred_element_type=F32)
 
 
-def rest_terms(idx, latents, b_left, e, w0):
-    tokens, f = latents.shape
+def rest_terms(idx, high, low, b_left, e, w0):
+    f, tokens = high.shape
     width = e.shape[1]
     half = width // 2
+    whole = pl.BlockSpec((f, tokens), lambda i, s: (0, 0))
     kept = pl.BlockSpec((f, half // 2), lambda i, s: (0, i))
     return pl.pallas_call(
         rest_kernel,
@@ -221,38 +224,53 @@
             num_scalar_prefetch=1,
             grid=(2,),
             in_specs=[
-                pl.BlockSpec((tokens, f), lambda i, s: (0, 0)),
+                whole,
+                whole,
                 pl.BlockSpec((f, 2 * tokens), lambda i, s: (0, 0)),
                 pl.BlockSpec((tokens, width), lambda i, s: (0, 0)),
                 pl.BlockSpec((f // 2, width), lambda i, s: (i, 0)),
             ],
             out_specs=[kept, kept, pl.BlockSpec((tokens, f // 2), lambda i, s: (0, i))],
-            scratch_shapes=[pltpu.VMEM((f, 2 * tokens), BF)],
         ),
         out_shape=[jax.ShapeDtypeStruct((f, half), F32)] * 2 + [jax.ShapeDtypeStruct((tokens, f), F32)],
         compiler_params=params(40),
         cost_estimate=cost(6 * tokens * f * width, 16 << 20),
-    )(idx, latents, b_left, e, w0)
-
-
-def join_kernel(keep, come, scale, out):
-    out[...] = (keep[...] + wide(come[...]) * unit(scale[...])).astype(BF)
-
-
-def joined(keep, come):
-    f, width = keep.shape
-    tile = 256
-    block = pl.BlockSpec((tile, width), lambda i: (i, 0))
+    )(idx, high, low, b_left, e, w0)
+
+
+def join_kernel(idx, high, low, e, come, scale, out):
+    @pl.when(idx[0] < LAYERS - 1)
+    def _():
+        right = e[...]
+        keep = jnp.dot(high[...], right, preferred_element_type=F32) + jnp.dot(low[...], right, preferred_element_type=F32)
+        out[...] = (keep + wide(come[...]) * unit(scale[...])).astype(BF)
+
+
+def joined(idx, high, low, e, come):
+    f, tokens = high.shape
+    width = e.shape[1]
+    tile = width // 2
+    whole = pl.BlockSpec((f, tokens), lambda i, s: (0, 0))
+    block = pl.BlockSpec((f, tile), lambda i, s: (0, i))
     return pl.pallas_call(
         join_kernel,
         name="join",
-        grid=(f // tile,),
-        in_specs=[block, block, pl.BlockSpec((SCALE_ROWS, width), lambda i: (f // SCALE_ROWS, 0))],
-        out_specs=block,
+        grid_spec=pltpu.PrefetchScalarGridSpec(
+            num_scalar_prefetch=1,
+            grid=(2,),
+            in_specs=[
+                whole,
+                whole,
+                pl.BlockSpec((tokens, tile), lambda i, s: (0, i)),
+                block,
+                pl.BlockSpec((SCALE_ROWS, tile), lambda i, s: (f // SCALE_ROWS, i)),
+            ],
+            out_specs=block,
+        ),
         out_shape=jax.ShapeDtypeStruct((f, width), BF),
         compiler_params=params(24),
-        cost_estimate=cost(4 * f * width, 4 << 20),
-    )(keep, come, come)
+        cost_estimate=cost(4 * tokens * f * width, 6 << 20),
+    )(idx, high, low, e, come, come)
 
 
 W_SUB = 64
@@ -303,7 +321,7 @@
                 pltpu.VMEM(((LAYERS - 1) * tile, width), BF),
             ],
         ),
-        out_shape=[jax.ShapeDtypeStruct((f, width), BF)] + [jax.ShapeDtypeStruct((tokens + SCALE_ROWS, f), I16)] * 3,
+        out_shape=[pltpu.HBM((f, width), BF)] + [jax.ShapeDtypeStruct((tokens + SCALE_ROWS, f), I16)] * 3,
         compiler_params=params(40),
         cost_estimate=cost(8 * tokens * f * width, 20 << 20),
     )(idx, e, decoder)
@@ -393,7 +411,7 @@
     other = jnp.where(place == 0, 2, 3)
     idx = jnp.stack([place, other, lax.axis_index("tok")]).astype(jnp.int32)
 
-    own_e, l_code, a_code, a_keep, o_code = first_terms(idx, errors, latents)
+    own_e, e_keep, high, low, l_code, a_code, o_code = first_terms(idx, errors, pltpu.with_memory_space_constraint(latents, pltpu.HBM))
     a_come = swapped(a_code)
     o_come = swapped(o_code)
     near = moved(l_code, group, [(0, 1), (1, 2)])
@@ -404,13 +422,13 @@
     two = moved(two_p, group, [(3, 1), (2, 0)])
     one = moved(one_p, group, [(3, 2), (2, 1), (1, 0)])
 
-    a_done = joined(a_keep, a_come)
+    a_done = joined(idx, high, low, e_keep, a_come)
     r_b = moved(a_done, group, [(2, 3)])
     r_a = moved(a_done, group, [(0, 2), (1, 3)])
 
     b_code, b_left = more_terms(idx, near, far, own_e)
     b_come = swapped(b_code)
-    o_keep, b_keep, own_p = rest_terms(idx, latents, b_left, own_e, w0)
+    o_keep, b_keep, own_p = rest_terms(idx, high, low, b_left, own_e, w0)
 
     latent_grad = gated(mask, own_p, (one, two, three))
     decoder_grad = weave(idx, o_keep, o_come, b_keep, b_come, r_a, r_b)

time: 116 us -> 113 us (0.974)
  local copies, waits for them, and re-layouts: 6.12 us -> 1.61 us
  Pallas kernels: 46.8 us -> 49.4 us
    unnamed x16 -> x14, local copies, waits for them, and re-layouts: 6.12 us -> 1.61 us
    pallas_call x1, Pallas kernels: 10.2 us -> 12.5 us  [first_terms(): pl.pallas_call(first_kernel, name='first_terms', grid_spec=pltpu.Prefetch...]
    ppermute x7, starting transfers between devices: 13.3 us -> 11.5 us  [moved(): lax.ppermute(array, 'dst', [(a * group + i, b * group + i) for a, b in pa...]
    ppermute x3, starting transfers between devices: 7.48 us -> 9.22 us  [swapped(): return lax.ppermute(array, 'tok', [(0, 1), (1, 0)])]
    pallas_call x1, Pallas kernels: 0.37 us -> 1.82 us  [joined(): pl.pallas_call(join_kernel, name='join', grid_spec=pltpu.PrefetchScalarGr...]
  transfers between devices with their start and end apart: 10 -> 10, of which waited for: 4 -> 4; matrix products, arithmetic and copies ran while one was open for 0% -> 0% of each run, Pallas kernels for 28% -> 30%
where the time goes in v2:
time: 113 us
  Pallas kernels  49.4 us (44%)
  waiting for transfers between devices  40 us (35%)
  starting transfers between devices  20.7 us (18%)
  local copies, waits for them, and re-layouts  1.61 us (1%)
    ppermute x7, waiting for transfers between devices, moved(): lax.ppermute(array, 'dst', [(a * group + i, b * group + i) for a, b in pa...  40 us
    pallas_call x1, Pallas kernels, partials(): pl.pallas_call(partial_kernel, name='partials', grid_spec=pltpu.PrefetchS...  14.8 us
    pallas_call x1, Pallas kernels, first_terms(): pl.pallas_call(first_kernel, name='first_terms', grid_spec=pltpu.Prefetch...  12.5 us
    ppermute x7, starting transfers between devices, moved(): lax.ppermute(array, 'dst', [(a * group + i, b * group + i) for a, b in pa...  11.5 us
    pallas_call x1, Pallas kernels, rest_terms(): pl.pallas_call(rest_kernel, name='rest_terms', grid_spec=pltpu.PrefetchSc...  10.1 us
    ppermute x3, starting transfers between devices, swapped(): return lax.ppermute(array, 'tok', [(0, 1), (1, 0)])  9.22 us
    pallas_call x1, Pallas kernels, more_terms(): pl.pallas_call(more_kernel, name='more_terms', grid_spec=pltpu.PrefetchSc...  4.5 us
    pallas_call x1, Pallas kernels, weave(): pl.pallas_call(weave_kernel, name='weave', grid_spec=pltpu.PrefetchScalar...  3.7 us
  transfers between devices with their start and end apart: 10, of which 4 were waited for; matrix products, arithmetic and copies ran while one was open for 0% of the time, Pallas kernels for 30%

profile of v2, /device:TPU:6, one launch (start us, length us, event | category | flops | bytes accessed | tf_op | source)
XLA Modules:
  0.0 112.5 jit_solution(14153252367290524011)
XLA Ops:
  0.6 0.1 pad_add_fusion.idx
  0.7 12.5 %first_terms.1 = (bf16[1024,2048]{1,0:T(8,128)(2,1)S(1)}, bf16[1024,1024]{1,0:T(8,128)(2,1)}, bf16[512,1024]{1,0:T(8,128)(2,1)}, bf16[512,1024]{1,0:T(8,128)(2,1...) custom-call(s32[3]{0:T(128)S(1)} %pad_add_fusion.idx, ...), custom_call_target="tpu_custom_call" | custom-call | flops 17179869184 | bytes 31457280 | tf_op jit(solution)/shard_map/first_terms/pallas_call | solution.py:117
  13.2 1.3 %collective-permute-start.1 = (s16[1032,512]{1,0:T(8,128)(2,1)S(1)}, s16[1032,512]{1,0:T(8,128)(2,1)S(1)}, u32[]{:S(2)}, u32[]{:S(2)}) collective-permute-start(s16[1032,512]{1,0:T(8,128)(2,1)S(1)} %get-tuple-element.20), channel_id=1, source_target_pairs={{0,96},{2,98},{4,100},{6,102},{8,104},{10,106},{12,108},{14,110},{... | collective-permute-start | bytes 3170312 | tf_op jit(solution)/shard_map/ppermute | solution.py:377
  14.5 0.7 collective-permute-start
  15.2 3.5 %collective-permute-start.4 = (s16[520,1024]{1,0:T(8,128)(2,1)S(1)}, s16[520,1024]{1,0:T(8,128)(2,1)S(1)}, u32[]{:S(2)}, u32[]{:S(2)}) collective-permute-start(s16[520,1024]{1,0:T(8,128)(2,1)S(1)} %get-tuple-element.29), channel_id=1, source_target_pairs={{0,1},{1,0},{2,3},{3,2},{4,5},{5,4},{6,7},{7,6},{8,9},{9,8},{10,11... | collective-permute-start | bytes 3194888 | tf_op jit(solution)/shard_map/ppermute | solution.py:381
  18.7 14.8 %partials.1 = (bf16[512,2048]{1,0:T(8,128)(2,1)}, s16[1032,512]{1,0:T(8,128)(2,1)S(1)}, s16[1032,512]{1,0:T(8,128)(2,1)S(1)}, s16[1032,512]{1,0:T(8,128)(2,1)}) custom-call(s32[3]{0:T(128)S(1)} %pad_add_fusion.idx, bf16[1024,2048]{1,0:T(8,128)(2,1)S(1)} %get-tuple-element.21.e, bf16[512,4,2048]{2,1,0:T(4,128)(2,1)} %w.1), custom_call_target="tpu_custom_call" | custom-call | flops 8589934592 | bytes 20971520 | tf_op jit(solution)/shard_map/partials/pallas_call | solution.py:308
  33.5 2.9 %collective-permute-start.7 = (s16[1032,512]{1,0:T(8,128)(2,1)S(1)}, s16[1032,512]{1,0:T(8,128)(2,1)S(1)}, u32[]{:S(2)}, u32[]{:S(2)}) collective-permute-start(s16[1032,512]{1,0:T(8,128)(2,1)S(1)} %get-tuple-element.31), channel_id=1, source_target_pairs={{96,64},{98,66},{100,68},{102,70},{104,72},{106,74},{108,76},{110,... | collective-permute-start | bytes 3170312 | tf_op jit(solution)/shard_map/ppermute | solution.py:377
  36.5 1.8 %collective-permute-start.8 = (s16[1032,512]{1,0:T(8,128)(2,1)S(1)}, s16[1032,512]{1,0:T(8,128)(2,1)S(1)}, u32[]{:S(2)}, u32[]{:S(2)}) collective-permute-start(s16[1032,512]{1,0:T(8,128)(2,1)S(1)} %get-tuple-element.32), channel_id=1, source_target_pairs={{96,32},{98,34},{100,36},{102,38},{104,40},{106,42},{108,44},{110,... | collective-permute-start | bytes 3170312 | tf_op jit(solution)/shard_map/ppermute | solution.py:377
  38.3 3.1 %collective-permute-done.1.far = s16[1032,512]{1,0:T(8,128)(2,1)S(1)} collective-permute-done((s16[1032,512]{1,0:T(8,128)(2,1)S(1)}, s16[1032,512]{1,0:T(8,128)(2,1)S(1)}, u32[]{:S(2)}, u32[]{:S(2)}) %collective-permute-start.1) | collective-permute-done | bytes 1056800 | tf_op jit(solution)/shard_map/ppermute | solution.py:377
  41.4 3.3 %collective-permute-start.2 = (s16[520,1024]{1,0:T(8,128)(2,1)S(1)}, s16[520,1024]{1,0:T(8,128)(2,1)S(1)}, u32[]{:S(2)}, u32[]{:S(2)}) collective-permute-start(s16[520,1024]{1,0:T(8,128)(2,1)S(1)} %get-tuple-element.25), channel_id=1, source_target_pairs={{0,1},{1,0},{2,3},{3,2},{4,5},{5,4},{6,7},{7,6},{8,9},{9,8},{10,11... | collective-permute-start | bytes 3194888 | tf_op jit(solution)/shard_map/ppermute | solution.py:381
  44.7 0.0 collective-permute-done.near
  44.7 1.9 %collective-permute-start.9 = (s16[1032,512]{1,0:T(8,128)(2,1)}, s16[1032,512]{1,0:T(8,128)(2,1)S(1)}, u32[]{:S(2)}, u32[]{:S(2)}) collective-permute-start(s16[1032,512]{1,0:T(8,128)(2,1)} %get-tuple-element.33), channel_id=1, source_target_pairs={{96,0},{98,2},{100,4},{102,6},{104,8},{106,10},{108,12},{110,14},{... | collective-permute-start | bytes 3170312 | tf_op jit(solution)/shard_map/ppermute | solution.py:377
  46.6 0.0 copy-done.5
  46.6 4.5 %more_terms.1 = (s16[520,1024]{1,0:T(8,128)(2,1)S(1)}, bf16[512,2048]{1,0:T(8,128)(2,1)S(1)}) custom-call(s32[3]{0:T(128)S(1)} %pad_add_fusion.idx, s16[1032,512]{1,0:T(8,128)(2,1)S(1)} %collective-permute-done.near, s16[1032,512]{1,0:T(8,128)(2,1)S(1)} %collective-permute-done.1.far, bf16[1024,2048]{1,0:T(8,128)(2,1)S(1)} %get-tuple-element.21.e), custom_call_target="tpu_custom_call" | custom-call | flops 2147483648 | bytes 8388608 | tf_op jit(solution)/shard_map/more_terms/pallas_call | solution.py:177
  51.1 0.0 collective-permute-done.4.come.scale
  51.1 2.5 %collective-permute-start.3 = (s16[520,1024]{1,0:T(8,128)(2,1)S(1)}, s16[520,1024]{1,0:T(8,128)(2,1)S(1)}, u32[]{:S(2)}, u32[]{:S(2)}) collective-permute-start(s16[520,1024]{1,0:T(8,128)(2,1)S(1)} %get-tuple-element.27), channel_id=1, source_target_pairs={{0,1},{1,0},{2,3},{3,2},{4,5},{5,4},{6,7},{7,6},{8,9},{9,8},{10,11... | collective-permute-start | bytes 3194888 | tf_op jit(solution)/shard_map/ppermute | solution.py:381
  53.6 0.0 copy-done.1
  53.6 0.0 copy-done.4
  53.6 1.8 %join.1 = bf16[512,1024]{1,0:T(8,128)(2,1)} custom-call(s32[3]{0:T(128)S(1)} %pad_add_fusion.idx, bf16[512,1024]{1,0:T(8,128)(2,1)S(1)} %copy-done.2, bf16[512,1024]{1,0:T(8,128)(2,1)S(1)} %copy-done.4, bf16[1024,1024]{1,0:T(8,128)(2,1)S(1)} %copy-done.1, s16[520,1024]{1,0:T(8,128)(2,1)S(1)} %collective-permute-done.4.come.scale, ...), custom_call_target="tpu_custom_call" | custom-call | flops 2147483648 | bytes 6291456 | tf_op jit(solution)/shard_map/join/pallas_call | solution.py:255
  55.4 4.7 %collective-permute-done.7.one.one_scale = s16[1032,512]{1,0:T(8,128)(2,1)S(1)} collective-permute-done((s16[1032,512]{1,0:T(8,128)(2,1)S(1)}, s16[1032,512]{1,0:T(8,128)(2,1)S(1)}, u32[]{:S(2)}, u32[]{:S(2)}) %collective-permute-start.7) | collective-permute-done | bytes 1056800 | tf_op jit(solution)/shard_map/ppermute | solution.py:377
  60.1 1.3 %collective-permute-start.6 = (bf16[512,1024]{1,0:T(8,128)(2,1)}, bf16[512,1024]{1,0:T(8,128)(2,1)S(1)}, u32[]{:S(2)}, u32[]{:S(2)}) collective-permute-start(bf16[512,1024]{1,0:T(8,128)(2,1)} %join.1), channel_id=1, source_target_pairs={{64,96},{66,98},{68,100},{70,102},{72,104},{74,106},{76,108},{78,1... | collective-permute-start | bytes 3145736 | tf_op jit(solution)/shard_map/ppermute | solution.py:377
  61.4 19.9 %collective-permute-done.8.two.two_scale = s16[1032,512]{1,0:T(8,128)(2,1)S(1)} collective-permute-done((s16[1032,512]{1,0:T(8,128)(2,1)S(1)}, s16[1032,512]{1,0:T(8,128)(2,1)S(1)}, u32[]{:S(2)}, u32[]{:S(2)}) %collective-permute-start.8) | collective-permute-done | bytes 1056800 | tf_op jit(solution)/shard_map/ppermute | solution.py:377
  81.3 1.5 %collective-permute-start.5 = (bf16[512,1024]{1,0:T(8,128)(2,1)}, bf16[512,1024]{1,0:T(8,128)(2,1)S(1)}, u32[]{:S(2)}, u32[]{:S(2)}) collective-permute-start(bf16[512,1024]{1,0:T(8,128)(2,1)} %join.1), channel_id=1, source_target_pairs={{0,64},{2,66},{4,68},{6,70},{8,72},{10,74},{12,76},{14,78},{16,80}... | collective-permute-start | bytes 3145736 | tf_op jit(solution)/shard_map/ppermute | solution.py:377
  82.9 1.6 %copy-done.6 = bf16[512,2048]{1,0:T(8,128)(2,1)S(1)} copy-done((bf16[512,2048]{1,0:T(8,128)(2,1)S(1)}, bf16[512,2048]{1,0:T(8,128)(2,1)}, u32[]{:S(2)}) %copy-start.6) | copy-done | bytes 2097176
  84.5 10.1 %rest_terms.1 = (f32[512,1024]{1,0:T(8,128)S(1)}, f32[512,1024]{1,0:T(8,128)S(1)}, f32[1024,512]{1,0:T(8,128)S(1)}) custom-call(s32[3]{0:T(128)S(1)} %pad_add_fusion.idx, bf16[512,1024]{1,0:T(8,128)(2,1)S(1)} %copy-done.3, bf16[512,1024]{1,0:T(8,128)(2,1)S(1)} %copy-done.4, bf16[512,2048]{1,0:T(8,128)(2,1)S(1)} %get-tuple-element.22.b_left, ...), custom_call_target="tpu_custom_call" | custom-call | flops 6442450944 | bytes 16777216 | tf_op jit(solution)/shard_map/rest_terms/pallas_call | solution.py:220
  94.5 0.0 collective-permute-done.9.three.three_scale
  94.6 2.0 %gate.1 = f32[1024,512]{1,0:T(8,128)} custom-call(s32[1024,512]{1,0:T(8,128)S(1)} %copy-done, f32[1024,512]{1,0:T(8,128)S(1)} %get-tuple-element.30.own, s16[1032,512]{1,0:T(8,128)(2,1)S(1)} %collective-permute-done.7.one.one_scale, s16[1032,512]{1,0:T(8,128)(2,1)S(1)} %collective-permute-done.8.two.two_scale, ...), custom_call_target="tpu_custom_call" | custom-call | flops 4194304 | bytes 9437184 | tf_op jit(solution)/shard_map/gate/pallas_call | solution.py:396
  96.5 0.0 collective-permute-done.2.o_come.o_scale
  96.5 0.0 collective-permute-done.6.r_b
  96.5 12.3 %collective-permute-done.5.r_a = bf16[512,1024]{1,0:T(8,128)(2,1)S(1)} collective-permute-done((bf16[512,1024]{1,0:T(8,128)(2,1)}, bf16[512,1024]{1,0:T(8,128)(2,1)S(1)}, u32[]{:S(2)}, u32[]{:S(2)}) %collective-permute-start.5) | collective-permute-done | bytes 1048608 | tf_op jit(solution)/shard_map/ppermute | solution.py:377
  108.8 0.0 collective-permute-done.3.b_come.b_scale
  108.8 3.7 %weave.1 = bf16[512,4,1024]{2,1,0:T(4,128)(2,1)} custom-call(s32[3]{0:T(128)S(1)} %pad_add_fusion.idx, f32[512,1024]{1,0:T(8,128)S(1)} %get-tuple-element.24.o_keep, s16[520,1024]{1,0:T(8,128)(2,1)S(1)} %collective-permute-done.2.o_come.o_scale, s16[520,1024]{1,0:T(8,128)(2,1)S(1)} %collective-permute-done.2.o_come.o_scale, ...), custom_call_target="tpu_custom_call" | custom-call | flops 1073741824 | bytes 8388608 | tf_op jit(solution)/shard_map/weave/pallas_call | solution.py:360
  (10 shorter events, 0.0 us)
Async XLA Ops:
  13.2 33.4 %copy-start.5 = (bf16[1024,2048]{1,0:T(8,128)(2,1)}, bf16[1024,2048]{1,0:T(8,128)(2,1)S(1)}, u32[]{:S(2)}) copy-start(bf16[1024,2048]{1,0:T(8,128)(2,1)S(1)} %get-tuple-element.21.e) | copy-start | bytes 12582916
  13.2 28.2 %collective-permute-start.1 = (s16[1032,512]{1,0:T(8,128)(2,1)S(1)}, s16[1032,512]{1,0:T(8,128)(2,1)S(1)}, u32[]{:S(2)}, u32[]{:S(2)}) collective-permute-start(s16[1032,512]{1,0:T(8,128)(2,1)S(1)} %get-tuple-element.20), channel_id=1, source_target_pairs={{0,96},{2,98},{4,100},{6,102},{8,104},{10,106},{12,108},{14,110},{... | collective-permute-start | bytes 3170312 | tf_op jit(solution)/shard_map/ppermute | solution.py:377
  14.5 30.2 %collective-permute-start = (s16[1032,512]{1,0:T(8,128)(2,1)S(1)}, s16[1032,512]{1,0:T(8,128)(2,1)S(1)}, u32[]{:S(2)}, u32[]{:S(2)}) collective-permute-start(s16[1032,512]{1,0:T(8,128)(2,1)S(1)} %get-tuple-element.20), channel_id=1, source_target_pairs={{0,32},{2,34},{4,36},{6,38},{8,40},{10,42},{12,44},{14,46},{16,48}... | collective-permute-start | bytes 3170312 | tf_op jit(solution)/shard_map/ppermute | solution.py:377
  15.2 35.9 %collective-permute-start.4 = (s16[520,1024]{1,0:T(8,128)(2,1)S(1)}, s16[520,1024]{1,0:T(8,128)(2,1)S(1)}, u32[]{:S(2)}, u32[]{:S(2)}) collective-permute-start(s16[520,1024]{1,0:T(8,128)(2,1)S(1)} %get-tuple-element.29), channel_id=1, source_target_pairs={{0,1},{1,0},{2,3},{3,2},{4,5},{5,4},{6,7},{7,6},{8,9},{9,8},{10,11... | collective-permute-start | bytes 3194888 | tf_op jit(solution)/shard_map/ppermute | solution.py:381
  33.5 26.6 %collective-permute-start.7 = (s16[1032,512]{1,0:T(8,128)(2,1)S(1)}, s16[1032,512]{1,0:T(8,128)(2,1)S(1)}, u32[]{:S(2)}, u32[]{:S(2)}) collective-permute-start(s16[1032,512]{1,0:T(8,128)(2,1)S(1)} %get-tuple-element.31), channel_id=1, source_target_pairs={{96,64},{98,66},{100,68},{102,70},{104,72},{106,74},{108,76},{110,... | collective-permute-start | bytes 3170312 | tf_op jit(solution)/shard_map/ppermute | solution.py:377
  36.5 44.9 %collective-permute-start.8 = (s16[1032,512]{1,0:T(8,128)(2,1)S(1)}, s16[1032,512]{1,0:T(8,128)(2,1)S(1)}, u32[]{:S(2)}, u32[]{:S(2)}) collective-permute-start(s16[1032,512]{1,0:T(8,128)(2,1)S(1)} %get-tuple-element.32), channel_id=1, source_target_pairs={{96,32},{98,34},{100,36},{102,38},{104,40},{106,42},{108,44},{110,... | collective-permute-start | bytes 3170312 | tf_op jit(solution)/shard_map/ppermute | solution.py:377
  41.4 55.2 %collective-permute-start.2 = (s16[520,1024]{1,0:T(8,128)(2,1)S(1)}, s16[520,1024]{1,0:T(8,128)(2,1)S(1)}, u32[]{:S(2)}, u32[]{:S(2)}) collective-permute-start(s16[520,1024]{1,0:T(8,128)(2,1)S(1)} %get-tuple-element.25), channel_id=1, source_target_pairs={{0,1},{1,0},{2,3},{3,2},{4,5},{5,4},{6,7},{7,6},{8,9},{9,8},{10,11... | collective-permute-start | bytes 3194888 | tf_op jit(solution)/shard_map/ppermute | solution.py:381
  44.7 8.9 %copy-start.1 = (bf16[1024,1024]{1,0:T(8,128)(2,1)S(1)}, bf16[1024,1024]{1,0:T(8,128)(2,1)}, u32[]{:S(2)}) copy-start(bf16[1024,1024]{1,0:T(8,128)(2,1)} %get-tuple-element.28.e) | copy-start | bytes 6291460
  44.7 8.9 %copy-start.2 = (bf16[512,1024]{1,0:T(8,128)(2,1)S(1)}, bf16[512,1024]{1,0:T(8,128)(2,1)}, u32[]{:S(2)}) copy-start(bf16[512,1024]{1,0:T(8,128)(2,1)} %get-tuple-element.18.high) | copy-start | bytes 3145732
  44.7 8.9 %copy-start.4 = (bf16[512,1024]{1,0:T(8,128)(2,1)S(1)}, bf16[512,1024]{1,0:T(8,128)(2,1)}, u32[]{:S(2)}) copy-start(bf16[512,1024]{1,0:T(8,128)(2,1)} %get-tuple-element.19.low) | copy-start | bytes 3145732
  44.7 49.9 %collective-permute-start.9 = (s16[1032,512]{1,0:T(8,128)(2,1)}, s16[1032,512]{1,0:T(8,128)(2,1)S(1)}, u32[]{:S(2)}, u32[]{:S(2)}) collective-permute-start(s16[1032,512]{1,0:T(8,128)(2,1)} %get-tuple-element.33), channel_id=1, source_target_pairs={{96,0},{98,2},{100,4},{102,6},{104,8},{106,10},{108,12},{110,14},{... | collective-permute-start | bytes 3170312 | tf_op jit(solution)/shard_map/ppermute | solution.py:377
  51.1 57.7 %collective-permute-start.3 = (s16[520,1024]{1,0:T(8,128)(2,1)S(1)}, s16[520,1024]{1,0:T(8,128)(2,1)S(1)}, u32[]{:S(2)}, u32[]{:S(2)}) collective-permute-start(s16[520,1024]{1,0:T(8,128)(2,1)S(1)} %get-tuple-element.27), channel_id=1, source_target_pairs={{0,1},{1,0},{2,3},{3,2},{4,5},{5,4},{6,7},{7,6},{8,9},{9,8},{10,11... | collective-permute-start | bytes 3194888 | tf_op jit(solution)/shard_map/ppermute | solution.py:381
  53.6 29.2 %copy-start.3 = (bf16[512,1024]{1,0:T(8,128)(2,1)S(1)}, bf16[512,1024]{1,0:T(8,128)(2,1)}, u32[]{:S(2)}) copy-start(bf16[512,1024]{1,0:T(8,128)(2,1)} %get-tuple-element.18.high) | copy-start | bytes 3145732
  60.1 36.4 %collective-permute-start.6 = (bf16[512,1024]{1,0:T(8,128)(2,1)}, bf16[512,1024]{1,0:T(8,128)(2,1)S(1)}, u32[]{:S(2)}, u32[]{:S(2)}) collective-permute-start(bf16[512,1024]{1,0:T(8,128)(2,1)} %join.1), channel_id=1, source_target_pairs={{64,96},{66,98},{68,100},{70,102},{72,104},{74,106},{76,108},{78,1... | collective-permute-start | bytes 3145736 | tf_op jit(solution)/shard_map/ppermute | solution.py:377
  81.3 27.5 %collective-permute-start.5 = (bf16[512,1024]{1,0:T(8,128)(2,1)}, bf16[512,1024]{1,0:T(8,128)(2,1)S(1)}, u32[]{:S(2)}, u32[]{:S(2)}) collective-permute-start(bf16[512,1024]{1,0:T(8,128)(2,1)} %join.1), channel_id=1, source_target_pairs={{0,64},{2,66},{4,68},{6,70},{8,72},{10,74},{12,76},{14,78},{16,80}... | collective-permute-start | bytes 3145736 | tf_op jit(solution)/shard_map/ppermute | solution.py:377
  82.9 1.6 %copy-start.6 = (bf16[512,2048]{1,0:T(8,128)(2,1)S(1)}, bf16[512,2048]{1,0:T(8,128)(2,1)}, u32[]{:S(2)}) copy-start(bf16[512,2048]{1,0:T(8,128)(2,1)} %get-tuple-element.23.w0) | copy-start | bytes 6291460
  84.5 10.1 %copy-start = (s32[1024,512]{1,0:T(8,128)S(1)}, s32[1024,512]{1,0:T(8,128)}, u32[]{:S(2)}) copy-start(s32[1024,512]{1,0:T(8,128)} %mask.1) | copy-start | bytes 6291460

commit v3 on v2

--- a/solution.py
+++ b/solution.py
@@ -59,7 +59,7 @@
 SUB = 64
 
 
-def first_kernel(idx, er, lat, own_e, e_keep, high, low, l_code, a_code, o_code, pick, e_a, a_send, o_send):
+def first_kernel(idx, er, lat, own_e, e_keep, high, low, l_code, a_code, pick, e_a, a_send):
     step = pl.program_id(0)
     tokens, _, width = er.shape
     half = width // 2
@@ -86,7 +86,6 @@
         term = jnp.dot(left, jnp.concatenate([right, right], axis=0), preferred_element_type=F32)
         out[...] = term + jnp.where(step > 0, out[...], 0.0)
 
-    add(o_send, own_e, send_at)
 
     @pl.when(early)
     def _():
@@ -96,10 +95,6 @@
     @pl.when(last & early)
     def _():
         encode(a_send[...], a_code)
-
-    @pl.when(last)
-    def _():
-        encode(o_send[...], o_code)
 
     @pl.when(last & (idx[0] < 2))
     def _():
@@ -131,12 +126,10 @@
                 left,
                 pl.BlockSpec((tokens + SCALE_ROWS, f), lambda i, s: (0, 0)),
                 whole_code,
-                whole_code,
             ],
             scratch_shapes=[
                 pltpu.VMEM((2 * SUB, LAYERS * SUB), BF),
                 pltpu.VMEM((tile, width), BF),
-                pltpu.VMEM((f, half), F32),
                 pltpu.VMEM((f, half), F32),
             ],
         ),
@@ -147,11 +140,35 @@
             shape,
             jax.ShapeDtypeStruct((tokens + SCALE_ROWS, f), I16),
             code,
-            code,
         ],
         compiler_params=params(38),
         cost_estimate=cost(16 * tokens * f * width, 30 << 20),
     )(idx, errors, latents)
+
+
+def own_kernel(idx, high, low, e, code):
+    right = e[...]
+    encode(jnp.dot(high[...], right, preferred_element_type=F32) + jnp.dot(low[...], right, preferred_element_type=F32), code)
+
+
+def own_terms(idx, high, low, e):
+    f, tokens = high.shape
+    half = e.shape[1] // 2
+    tile = half // 2
+    whole = pl.BlockSpec((f, tokens), lambda i, s: (0, 0))
+    return pl.pallas_call(
+        own_kernel,
+        name="own_terms",
+        grid_spec=pltpu.PrefetchScalarGridSpec(
+            num_scalar_prefetch=1,
+            grid=(2,),
+            in_specs=[whole, whole, pl.BlockSpec((tokens, tile), lambda i, s: (0, i + 2 * (1 - s[2])))],
+            out_specs=pl.BlockSpec((f + SCALE_ROWS, tile), lambda i, s: (0, i)),
+        ),
+        out_shape=jax.ShapeDtypeStruct((f + SCALE_ROWS, half), I16),
+        compiler_params=params(24),
+        cost_estimate=cost(4 * tokens * f * half, 6 << 20),
+    )(idx, high, low, e)
 
 
 def more_kernel(idx, near, far, e, code, left):
@@ -411,15 +428,16 @@
     other = jnp.where(place == 0, 2, 3)
     idx = jnp.stack([place, other, lax.axis_index("tok")]).astype(jnp.int32)
 
-    own_e, e_keep, high, low, l_code, a_code, o_code = first_terms(idx, errors, pltpu.with_memory_space_constraint(latents, pltpu.HBM))
+    own_e, e_keep, high, low, l_code, a_code = first_terms(idx, errors, pltpu.with_memory_space_constraint(latents, pltpu.HBM))
     a_come = swapped(a_code)
-    o_come = swapped(o_code)
     near = moved(l_code, group, [(0, 1), (1, 2)])
     far = moved(l_code, group, [(0, 3)])
 
     w0, one_p, two_p, three_p = partials(idx, own_e, decoder)
     three = moved(three_p, group, [(3, 0)])
     two = moved(two_p, group, [(3, 1), (2, 0)])
+    o_code = own_terms(idx, high, low, own_e)
+    o_come = swapped(o_code)
     one = moved(one_p, group, [(3, 2), (2, 1), (1, 0)])
 
     a_done = joined(idx, high, low, e_keep, a_come)

time: 113 us -> 110 us (0.973)
  the two profiles are of different devices: /device:TPU:6 before, /device:TPU:38 now
where the time goes in v3:
time: 110 us
  Pallas kernels  51.2 us (47%)
  waiting for transfers between devices  35.4 us (32%)
  starting transfers between devices  19.3 us (18%)
  local copies, waits for them, and re-layouts  3.2 us (3%)
    ppermute x7, waiting for transfers between devices, moved(): lax.ppermute(array, 'dst', [(a * group + i, b * group + i) for a, b in pa...  35.4 us
    pallas_call x1, Pallas kernels, partials(): pl.pallas_call(partial_kernel, name='partials', grid_spec=pltpu.PrefetchS...  14.9 us
    ppermute x7, starting transfers between devices, moved(): lax.ppermute(array, 'dst', [(a * group + i, b * group + i) for a, b in pa...  10.9 us
    pallas_call x1, Pallas kernels, first_terms(): pl.pallas_call(first_kernel, name='first_terms', grid_spec=pltpu.Prefetch...  10.3 us
    pallas_call x1, Pallas kernels, rest_terms(): pl.pallas_call(rest_kernel, name='rest_terms', grid_spec=pltpu.PrefetchSc...  10.1 us
    ppermute x3, starting transfers between devices, swapped(): return lax.ppermute(array, 'tok', [(0, 1), (1, 0)])  8.38 us
    pallas_call x1, Pallas kernels, more_terms(): pl.pallas_call(more_kernel, name='more_terms', grid_spec=pltpu.PrefetchSc...  4.54 us
    pallas_call x1, Pallas kernels, own_terms(): pl.pallas_call(own_kernel, name='own_terms', grid_spec=pltpu.PrefetchScal...  3.81 us
  transfers between devices with their start and end apart: 10, of which 3 were waited for; matrix products, arithmetic and copies ran while one was open for 0% of the time, Pallas kernels for 34%

profile of v3, /device:TPU:38, one launch (start us, length us, event | category | flops | bytes accessed | tf_op | source)
XLA Modules:
  0.0 110.0 jit_solution(6970902849840312042)
XLA Ops:
  0.6 0.1 pad_add_fusion.idx
  0.7 10.3 %first_terms.1 = (bf16[1024,2048]{1,0:T(8,128)(2,1)S(1)}, bf16[1024,1024]{1,0:T(8,128)(2,1)}, bf16[512,1024]{1,0:T(8,128)(2,1)}, bf16[512,1024]{1,0:T(8,128)(2,1...) custom-call(s32[3]{0:T(128)S(1)} %pad_add_fusion.idx, bf16[1024,4,2048]{2,1,0:T(4,128)(2,1)} %er.1, ...), custom_call_target="tpu_custom_call" | custom-call | flops 17179869184 | bytes 31457280 | tf_op jit(solution)/shard_map/first_terms/pallas_call | solution.py:112
  11.1 1.3 %collective-permute-start.1 = (s16[1032,512]{1,0:T(8,128)(2,1)S(1)}, s16[1032,512]{1,0:T(8,128)(2,1)S(1)}, u32[]{:S(2)}, u32[]{:S(2)}) collective-permute-start(s16[1032,512]{1,0:T(8,128)(2,1)S(1)} %get-tuple-element.19), channel_id=1, source_target_pairs={{0,96},{2,98},{4,100},{6,102},{8,104},{10,106},{12,108},{14,110},{... | collective-permute-start | bytes 3170312 | tf_op jit(solution)/shard_map/ppermute | solution.py:394
  12.4 0.7 collective-permute-start
  13.1 3.3 %collective-permute-start.4 = (s16[520,1024]{1,0:T(8,128)(2,1)S(1)}, s16[520,1024]{1,0:T(8,128)(2,1)S(1)}, u32[]{:S(2)}, u32[]{:S(2)}) collective-permute-start(s16[520,1024]{1,0:T(8,128)(2,1)S(1)} %get-tuple-element.27), channel_id=1, source_target_pairs={{0,1},{1,0},{2,3},{3,2},{4,5},{5,4},{6,7},{7,6},{8,9},{9,8},{10,11... | collective-permute-start | bytes 3194888 | tf_op jit(solution)/shard_map/ppermute | solution.py:398
  16.4 14.9 %partials.1 = (bf16[512,2048]{1,0:T(8,128)(2,1)}, s16[1032,512]{1,0:T(8,128)(2,1)S(1)}, s16[1032,512]{1,0:T(8,128)(2,1)S(1)}, s16[1032,512]{1,0:T(8,128)(2,1)}) custom-call(s32[3]{0:T(128)S(1)} %pad_add_fusion.idx, bf16[1024,2048]{1,0:T(8,128)(2,1)S(1)} %get-tuple-element.20.e, bf16[512,4,2048]{2,1,0:T(4,128)(2,1)} %w.1), custom_call_target="tpu_custom_call" | custom-call | flops 8589934592 | bytes 20971520 | tf_op jit(solution)/shard_map/partials/pallas_call | solution.py:325
  31.3 2.7 %collective-permute-start.7 = (s16[1032,512]{1,0:T(8,128)(2,1)S(1)}, s16[1032,512]{1,0:T(8,128)(2,1)S(1)}, u32[]{:S(2)}, u32[]{:S(2)}) collective-permute-start(s16[1032,512]{1,0:T(8,128)(2,1)S(1)} %get-tuple-element.29), channel_id=1, source_target_pairs={{96,64},{98,66},{100,68},{102,70},{104,72},{106,74},{108,76},{110,... | collective-permute-start | bytes 3170312 | tf_op jit(solution)/shard_map/ppermute | solution.py:394
  33.9 2.0 %collective-permute-start.8 = (s16[1032,512]{1,0:T(8,128)(2,1)S(1)}, s16[1032,512]{1,0:T(8,128)(2,1)S(1)}, u32[]{:S(2)}, u32[]{:S(2)}) collective-permute-start(s16[1032,512]{1,0:T(8,128)(2,1)S(1)} %get-tuple-element.30), channel_id=1, source_target_pairs={{96,32},{98,34},{100,36},{102,38},{104,40},{106,42},{108,44},{110,... | collective-permute-start | bytes 3170312 | tf_op jit(solution)/shard_map/ppermute | solution.py:394
  36.0 3.8 %own_terms.1 = s16[520,1024]{1,0:T(8,128)(2,1)S(1)} custom-call(s32[3]{0:T(128)S(1)} %pad_add_fusion.idx, bf16[512,1024]{1,0:T(8,128)(2,1)S(1)} %copy-done.3, bf16[512,1024]{1,0:T(8,128)(2,1)S(1)} %copy-done.5, bf16[1024,2048]{1,0:T(8,128)(2,1)S(1)} %get-tuple-element.20.e), custom_call_target="tpu_custom_call" | custom-call | flops 2147483648 | bytes 6291456 | tf_op jit(solution)/shard_map/own_terms/pallas_call | solution.py:159
  39.8 0.0 collective-permute-done.1.far
  39.8 2.6 %collective-permute-start.2 = (s16[520,1024]{1,0:T(8,128)(2,1)S(1)}, s16[520,1024]{1,0:T(8,128)(2,1)S(1)}, u32[]{:S(2)}, u32[]{:S(2)}) collective-permute-start(s16[520,1024]{1,0:T(8,128)(2,1)S(1)} %own_terms.1), channel_id=1, source_target_pairs={{0,1},{1,0},{2,3},{3,2},{4,5},{5,4},{6,7},{7,6},{8,9},{9,8},{10,11... | collective-permute-start | bytes 3194888 | tf_op jit(solution)/shard_map/ppermute | solution.py:398
  42.4 0.0 collective-permute-done.near
  42.4 1.6 %collective-permute-start.9 = (s16[1032,512]{1,0:T(8,128)(2,1)}, s16[1032,512]{1,0:T(8,128)(2,1)S(1)}, u32[]{:S(2)}, u32[]{:S(2)}) collective-permute-start(s16[1032,512]{1,0:T(8,128)(2,1)} %get-tuple-element.31), channel_id=1, source_target_pairs={{96,0},{98,2},{100,4},{102,6},{104,8},{106,10},{108,12},{110,14},{... | collective-permute-start | bytes 3170312 | tf_op jit(solution)/shard_map/ppermute | solution.py:394
  44.1 0.0 copy-done.1
  44.1 4.5 %more_terms.1 = (s16[520,1024]{1,0:T(8,128)(2,1)S(1)}, bf16[512,2048]{1,0:T(8,128)(2,1)S(1)}) custom-call(s32[3]{0:T(128)S(1)} %pad_add_fusion.idx, s16[1032,512]{1,0:T(8,128)(2,1)S(1)} %collective-permute-done.near, s16[1032,512]{1,0:T(8,128)(2,1)S(1)} %collective-permute-done.1.far, bf16[1024,2048]{1,0:T(8,128)(2,1)S(1)} %get-tuple-element.20.e), custom_call_target="tpu_custom_call" | custom-call | flops 2147483648 | bytes 8388608 | tf_op jit(solution)/shard_map/more_terms/pallas_call | solution.py:194
  48.7 0.0 collective-permute-done.4.come.scale
  48.7 2.5 %collective-permute-start.3 = (s16[520,1024]{1,0:T(8,128)(2,1)S(1)}, s16[520,1024]{1,0:T(8,128)(2,1)S(1)}, u32[]{:S(2)}, u32[]{:S(2)}) collective-permute-start(s16[520,1024]{1,0:T(8,128)(2,1)S(1)} %get-tuple-element.25), channel_id=1, source_target_pairs={{0,1},{1,0},{2,3},{3,2},{4,5},{5,4},{6,7},{7,6},{8,9},{9,8},{10,11... | collective-permute-start | bytes 3194888 | tf_op jit(solution)/shard_map/ppermute | solution.py:398
  51.2 1.9 %join.1 = bf16[512,1024]{1,0:T(8,128)(2,1)} custom-call(s32[3]{0:T(128)S(1)} %pad_add_fusion.idx, bf16[512,1024]{1,0:T(8,128)(2,1)S(1)} %copy-done.3, bf16[512,1024]{1,0:T(8,128)(2,1)S(1)} %copy-done.5, bf16[1024,1024]{1,0:T(8,128)(2,1)S(1)} %copy-done.2, s16[520,1024]{1,0:T(8,128)(2,1)S(1)} %collective-permute-done.4.come.scale, ...), custom_call_target="tpu_custom_call" | custom-call | flops 2147483648 | bytes 6291456 | tf_op jit(solution)/shard_map/join/pallas_call | solution.py:272
  53.0 4.6 %collective-permute-done.7.one.one_scale = s16[1032,512]{1,0:T(8,128)(2,1)S(1)} collective-permute-done((s16[1032,512]{1,0:T(8,128)(2,1)S(1)}, s16[1032,512]{1,0:T(8,128)(2,1)S(1)}, u32[]{:S(2)}, u32[]{:S(2)}) %collective-permute-start.7) | collective-permute-done | bytes 1056800 | tf_op jit(solution)/shard_map/ppermute | solution.py:394
  57.6 1.3 %collective-permute-start.6 = (bf16[512,1024]{1,0:T(8,128)(2,1)}, bf16[512,1024]{1,0:T(8,128)(2,1)S(1)}, u32[]{:S(2)}, u32[]{:S(2)}) collective-permute-start(bf16[512,1024]{1,0:T(8,128)(2,1)} %join.1), channel_id=1, source_target_pairs={{64,96},{66,98},{68,100},{70,102},{72,104},{74,106},{76,108},{78,1... | collective-permute-start | bytes 3145736 | tf_op jit(solution)/shard_map/ppermute | solution.py:394
  58.9 20.0 %collective-permute-done.8.two.two_scale = s16[1032,512]{1,0:T(8,128)(2,1)S(1)} collective-permute-done((s16[1032,512]{1,0:T(8,128)(2,1)S(1)}, s16[1032,512]{1,0:T(8,128)(2,1)S(1)}, u32[]{:S(2)}, u32[]{:S(2)}) %collective-permute-start.8) | collective-permute-done | bytes 1056800 | tf_op jit(solution)/shard_map/ppermute | solution.py:394
  78.8 1.3 %collective-permute-start.5 = (bf16[512,1024]{1,0:T(8,128)(2,1)}, bf16[512,1024]{1,0:T(8,128)(2,1)S(1)}, u32[]{:S(2)}, u32[]{:S(2)}) collective-permute-start(bf16[512,1024]{1,0:T(8,128)(2,1)} %join.1), channel_id=1, source_target_pairs={{0,64},{2,66},{4,68},{6,70},{8,72},{10,74},{12,76},{14,78},{16,80}... | collective-permute-start | bytes 3145736 | tf_op jit(solution)/shard_map/ppermute | solution.py:394
  80.1 1.6 %copy-done.8 = bf16[512,2048]{1,0:T(8,128)(2,1)S(1)} copy-done((bf16[512,2048]{1,0:T(8,128)(2,1)S(1)}, bf16[512,2048]{1,0:T(8,128)(2,1)}, u32[]{:S(2)}) %copy-start.8) | copy-done | bytes 2097176
  81.7 1.6 %copy-done.9 = bf16[512,2048]{1,0:T(8,128)(2,1)S(1)} copy-done((bf16[512,2048]{1,0:T(8,128)(2,1)S(1)}, bf16[512,2048]{1,0:T(8,128)(2,1)}, u32[]{:S(2)}) %copy-start.9) | copy-done | bytes 2097176
  83.3 10.1 %rest_terms.1 = (f32[512,1024]{1,0:T(8,128)S(1)}, f32[512,1024]{1,0:T(8,128)S(1)}, f32[1024,512]{1,0:T(8,128)S(1)}) custom-call(s32[3]{0:T(128)S(1)} %pad_add_fusion.idx, bf16[512,1024]{1,0:T(8,128)(2,1)S(1)} %copy-done.4, bf16[512,1024]{1,0:T(8,128)(2,1)S(1)} %copy-done.6, bf16[512,2048]{1,0:T(8,128)(2,1)S(1)} %copy-done.8, bf16[1024,2048]{1,0:T(8,128)(2,1)} %copy-done.1, ...), custom_call_target="tpu_custom_call" | custom-call | flops 6442450944 | bytes 16777216 | tf_op jit(solution)/shard_map/rest_terms/pallas_call | solution.py:237
  93.4 0.0 collective-permute-done.9.three.three_scale
  93.4 2.0 %gate.1 = f32[1024,512]{1,0:T(8,128)} custom-call(s32[1024,512]{1,0:T(8,128)S(1)} %copy-done, f32[1024,512]{1,0:T(8,128)S(1)} %get-tuple-element.28.own, s16[1032,512]{1,0:T(8,128)(2,1)S(1)} %collective-permute-done.7.one.one_scale, s16[1032,512]{1,0:T(8,128)(2,1)S(1)} %collective-permute-done.8.two.two_scale, ...), custom_call_target="tpu_custom_call" | custom-call | flops 4194304 | bytes 9437184 | tf_op jit(solution)/shard_map/gate/pallas_call | solution.py:413
  95.4 0.0 collective-permute-done.2.o_come.o_scale
  95.4 0.0 collective-permute-done.6.r_b
  95.4 10.9 %collective-permute-done.5.r_a = bf16[512,1024]{1,0:T(8,128)(2,1)S(1)} collective-permute-done((bf16[512,1024]{1,0:T(8,128)(2,1)}, bf16[512,1024]{1,0:T(8,128)(2,1)S(1)}, u32[]{:S(2)}, u32[]{:S(2)}) %collective-permute-start.5) | collective-permute-done | bytes 1048608 | tf_op jit(solution)/shard_map/ppermute | solution.py:394
  106.3 0.0 collective-permute-done.3.b_come.b_scale
  106.3 3.7 %weave.1 = bf16[512,4,1024]{2,1,0:T(4,128)(2,1)} custom-call(s32[3]{0:T(128)S(1)} %pad_add_fusion.idx, f32[512,1024]{1,0:T(8,128)S(1)} %get-tuple-element.23.o_keep, s16[520,1024]{1,0:T(8,128)(2,1)S(1)} %collective-permute-done.2.o_come.o_scale, s16[520,1024]{1,0:T(8,128)(2,1)S(1)} %collective-permute-done.2.o_come.o_scale, ...), custom_call_target="tpu_custom_call" | custom-call | flops 1073741824 | bytes 8388608 | tf_op jit(solution)/shard_map/weave/pallas_call | solution.py:377
  (17 shorter events, 0.0 us)
Async XLA Ops:
  11.1 33.0 %copy-start.1 = (bf16[1024,2048]{1,0:T(8,128)(2,1)}, bf16[1024,2048]{1,0:T(8,128)(2,1)S(1)}, u32[]{:S(2)}) copy-start(bf16[1024,2048]{1,0:T(8,128)(2,1)S(1)} %get-tuple-element.20.e) | copy-start | bytes 12582916
  11.1 28.7 %collective-permute-start.1 = (s16[1032,512]{1,0:T(8,128)(2,1)S(1)}, s16[1032,512]{1,0:T(8,128)(2,1)S(1)}, u32[]{:S(2)}, u32[]{:S(2)}) collective-permute-start(s16[1032,512]{1,0:T(8,128)(2,1)S(1)} %get-tuple-element.19), channel_id=1, source_target_pairs={{0,96},{2,98},{4,100},{6,102},{8,104},{10,106},{12,108},{14,110},{... | collective-permute-start | bytes 3170312 | tf_op jit(solution)/shard_map/ppermute | solution.py:394
  12.4 30.1 %collective-permute-start = (s16[1032,512]{1,0:T(8,128)(2,1)S(1)}, s16[1032,512]{1,0:T(8,128)(2,1)S(1)}, u32[]{:S(2)}, u32[]{:S(2)}) collective-permute-start(s16[1032,512]{1,0:T(8,128)(2,1)S(1)} %get-tuple-element.19), channel_id=1, source_target_pairs={{0,32},{2,34},{4,36},{6,38},{8,40},{10,42},{12,44},{14,46},{16,48}... | collective-permute-start | bytes 3170312 | tf_op jit(solution)/shard_map/ppermute | solution.py:394
  13.1 35.6 %collective-permute-start.4 = (s16[520,1024]{1,0:T(8,128)(2,1)S(1)}, s16[520,1024]{1,0:T(8,128)(2,1)S(1)}, u32[]{:S(2)}, u32[]{:S(2)}) collective-permute-start(s16[520,1024]{1,0:T(8,128)(2,1)S(1)} %get-tuple-element.27), channel_id=1, source_target_pairs={{0,1},{1,0},{2,3},{3,2},{4,5},{5,4},{6,7},{7,6},{8,9},{9,8},{10,11... | collective-permute-start | bytes 3194888 | tf_op jit(solution)/shard_map/ppermute | solution.py:398
  16.4 19.6 %copy-start.3 = (bf16[512,1024]{1,0:T(8,128)(2,1)S(1)}, bf16[512,1024]{1,0:T(8,128)(2,1)}, u32[]{:S(2)}) copy-start(bf16[512,1024]{1,0:T(8,128)(2,1)} %get-tuple-element.17.high) | copy-start | bytes 3145732
  16.4 19.6 %copy-start.5 = (bf16[512,1024]{1,0:T(8,128)(2,1)S(1)}, bf16[512,1024]{1,0:T(8,128)(2,1)}, u32[]{:S(2)}) copy-start(bf16[512,1024]{1,0:T(8,128)(2,1)} %get-tuple-element.18.low) | copy-start | bytes 3145732
  31.3 26.3 %collective-permute-start.7 = (s16[1032,512]{1,0:T(8,128)(2,1)S(1)}, s16[1032,512]{1,0:T(8,128)(2,1)S(1)}, u32[]{:S(2)}, u32[]{:S(2)}) collective-permute-start(s16[1032,512]{1,0:T(8,128)(2,1)S(1)} %get-tuple-element.29), channel_id=1, source_target_pairs={{96,64},{98,66},{100,68},{102,70},{104,72},{106,74},{108,76},{110,... | collective-permute-start | bytes 3170312 | tf_op jit(solution)/shard_map/ppermute | solution.py:394
  33.9 44.9 %collective-permute-start.8 = (s16[1032,512]{1,0:T(8,128)(2,1)S(1)}, s16[1032,512]{1,0:T(8,128)(2,1)S(1)}, u32[]{:S(2)}, u32[]{:S(2)}) collective-permute-start(s16[1032,512]{1,0:T(8,128)(2,1)S(1)} %get-tuple-element.30), channel_id=1, source_target_pairs={{96,32},{98,34},{100,36},{102,38},{104,40},{106,42},{108,44},{110,... | collective-permute-start | bytes 3170312 | tf_op jit(solution)/shard_map/ppermute | solution.py:394
  39.8 55.6 %collective-permute-start.2 = (s16[520,1024]{1,0:T(8,128)(2,1)S(1)}, s16[520,1024]{1,0:T(8,128)(2,1)S(1)}, u32[]{:S(2)}, u32[]{:S(2)}) collective-permute-start(s16[520,1024]{1,0:T(8,128)(2,1)S(1)} %own_terms.1), channel_id=1, source_target_pairs={{0,1},{1,0},{2,3},{3,2},{4,5},{5,4},{6,7},{7,6},{8,9},{9,8},{10,11... | collective-permute-start | bytes 3194888 | tf_op jit(solution)/shard_map/ppermute | solution.py:398
  42.4 8.7 %copy-start.2 = (bf16[1024,1024]{1,0:T(8,128)(2,1)S(1)}, bf16[1024,1024]{1,0:T(8,128)(2,1)}, u32[]{:S(2)}) copy-start(bf16[1024,1024]{1,0:T(8,128)(2,1)} %get-tuple-element.26.e) | copy-start | bytes 6291460
  42.4 51.0 %collective-permute-start.9 = (s16[1032,512]{1,0:T(8,128)(2,1)}, s16[1032,512]{1,0:T(8,128)(2,1)S(1)}, u32[]{:S(2)}, u32[]{:S(2)}) collective-permute-start(s16[1032,512]{1,0:T(8,128)(2,1)} %get-tuple-element.31), channel_id=1, source_target_pairs={{96,0},{98,2},{100,4},{102,6},{104,8},{106,10},{108,12},{110,14},{... | collective-permute-start | bytes 3170312 | tf_op jit(solution)/shard_map/ppermute | solution.py:394
  48.6 4.4 %copy-start.7 = (bf16[512,2048]{1,0:T(8,128)(2,1)}, bf16[512,2048]{1,0:T(8,128)(2,1)S(1)}, u32[]{:S(2)}) copy-start(bf16[512,2048]{1,0:T(8,128)(2,1)S(1)} %get-tuple-element.21.b_left) | copy-start | bytes 6291460
  48.7 57.7 %collective-permute-start.3 = (s16[520,1024]{1,0:T(8,128)(2,1)S(1)}, s16[520,1024]{1,0:T(8,128)(2,1)S(1)}, u32[]{:S(2)}, u32[]{:S(2)}) collective-permute-start(s16[520,1024]{1,0:T(8,128)(2,1)S(1)} %get-tuple-element.25), channel_id=1, source_target_pairs={{0,1},{1,0},{2,3},{3,2},{4,5},{5,4},{6,7},{7,6},{8,9},{9,8},{10,11... | collective-permute-start | bytes 3194888 | tf_op jit(solution)/shard_map/ppermute | solution.py:398
  51.1 29.0 %copy-start.4 = (bf16[512,1024]{1,0:T(8,128)(2,1)S(1)}, bf16[512,1024]{1,0:T(8,128)(2,1)}, u32[]{:S(2)}) copy-start(bf16[512,1024]{1,0:T(8,128)(2,1)} %get-tuple-element.17.high) | copy-start | bytes 3145732
  51.2 29.0 %copy-start.6 = (bf16[512,1024]{1,0:T(8,128)(2,1)S(1)}, bf16[512,1024]{1,0:T(8,128)(2,1)}, u32[]{:S(2)}) copy-start(bf16[512,1024]{1,0:T(8,128)(2,1)} %get-tuple-element.18.low) | copy-start | bytes 3145732
  57.6 37.8 %collective-permute-start.6 = (bf16[512,1024]{1,0:T(8,128)(2,1)}, bf16[512,1024]{1,0:T(8,128)(2,1)S(1)}, u32[]{:S(2)}, u32[]{:S(2)}) collective-permute-start(bf16[512,1024]{1,0:T(8,128)(2,1)} %join.1), channel_id=1, source_target_pairs={{64,96},{66,98},{68,100},{70,102},{72,104},{74,106},{76,108},{78,1... | collective-permute-start | bytes 3145736 | tf_op jit(solution)/shard_map/ppermute | solution.py:394
  78.8 27.5 %collective-permute-start.5 = (bf16[512,1024]{1,0:T(8,128)(2,1)}, bf16[512,1024]{1,0:T(8,128)(2,1)S(1)}, u32[]{:S(2)}, u32[]{:S(2)}) collective-permute-start(bf16[512,1024]{1,0:T(8,128)(2,1)} %join.1), channel_id=1, source_target_pairs={{0,64},{2,66},{4,68},{6,70},{8,72},{10,74},{12,76},{14,78},{16,80}... | collective-permute-start | bytes 3145736 | tf_op jit(solution)/shard_map/ppermute | solution.py:394
  80.1 1.6 %copy-start.8 = (bf16[512,2048]{1,0:T(8,128)(2,1)S(1)}, bf16[512,2048]{1,0:T(8,128)(2,1)}, u32[]{:S(2)}) copy-start(bf16[512,2048]{1,0:T(8,128)(2,1)} %copy-done.7) | copy-start | bytes 6291460
  81.7 1.6 %copy-start.9 = (bf16[512,2048]{1,0:T(8,128)(2,1)S(1)}, bf16[512,2048]{1,0:T(8,128)(2,1)}, u32[]{:S(2)}) copy-start(bf16[512,2048]{1,0:T(8,128)(2,1)} %get-tuple-element.22.w0) | copy-start | bytes 6291460
  83.3 10.1 %copy-start = (s32[1024,512]{1,0:T(8,128)S(1)}, s32[1024,512]{1,0:T(8,128)}, u32[]{:S(2)}) copy-start(s32[1024,512]{1,0:T(8,128)} %mask.1) | copy-start | bytes 6291460

commit v4 on v3

--- a/solution.py
+++ b/solution.py
@@ -216,19 +216,20 @@
     )(idx, near, far, e)
 
 
-def rest_kernel(idx, high, low, b_left, e, w0, o_keep, b_keep, own):
+def rest_kernel(idx, high, low, b_left, e, w0, o_come, o_scale, o_done, b_keep, own):
     step = pl.program_id(0)
-    _, tile = o_keep.shape
+    _, tile = o_done.shape
     half = e.shape[1] // 2
 
     right = e[:, pl.ds(pl.multiple_of(idx[2] * half + step * tile, tile), tile)]
-    o_keep[...] = jnp.dot(high[...], right, preferred_element_type=F32) + jnp.dot(low[...], right, preferred_element_type=F32)
+    o_keep = jnp.dot(high[...], right, preferred_element_type=F32) + jnp.dot(low[...], right, preferred_element_type=F32)
+    o_done[...] = (o_keep + wide(o_come[...]) * unit(o_scale[...])).astype(BF)
     right = jnp.concatenate([right, right], axis=0)
     b_keep[...] = jnp.dot(b_left[...], right, preferred_element_type=F32)
     own[...] = lax.dot_general(e[...], w0[...], (((1,), (1,)), ((), ())), preferred_element_type=F32)
 
 
-def rest_terms(idx, high, low, b_left, e, w0):
+def rest_terms(idx, high, low, b_left, e, w0, o_come):
     f, tokens = high.shape
     width = e.shape[1]
     half = width // 2
@@ -246,13 +247,19 @@
                 pl.BlockSpec((f, 2 * tokens), lambda i, s: (0, 0)),
                 pl.BlockSpec((tokens, width), lambda i, s: (0, 0)),
                 pl.BlockSpec((f // 2, width), lambda i, s: (i, 0)),
+                kept,
+                pl.BlockSpec((SCALE_ROWS, half // 2), lambda i, s: (f // SCALE_ROWS, i)),
             ],
             out_specs=[kept, kept, pl.BlockSpec((tokens, f // 2), lambda i, s: (0, i))],
         ),
-        out_shape=[jax.ShapeDtypeStruct((f, half), F32)] * 2 + [jax.ShapeDtypeStruct((tokens, f), F32)],
+        out_shape=[
+            jax.ShapeDtypeStruct((f, half), BF),
+            jax.ShapeDtypeStruct((f, half), F32),
+            jax.ShapeDtypeStruct((tokens, f), F32),
+        ],
         compiler_params=params(40),
         cost_estimate=cost(6 * tokens * f * width, 16 << 20),
-    )(idx, high, low, b_left, e, w0)
+    )(idx, high, low, b_left, e, w0, o_come, o_come)
 
 
 def join_kernel(idx, high, low, e, come, scale, out):
@@ -347,8 +354,8 @@
 WEAVE = 64
 
 
-def weave_kernel(idx, o_keep, o_come, o_scale, b_keep, b_come, b_scale, r_a, r_b, out, mix):
-    f, width = o_keep.shape
+def weave_kernel(idx, o_done, b_keep, b_come, b_scale, r_a, r_b, out, mix):
+    f, width = o_done.shape
     place = idx[0]
 
     @pl.when(pl.program_id(0) == 0)
@@ -360,18 +367,17 @@
     zero = jnp.zeros((WEAVE, width), BF)
     for j in range(f // WEAVE):
         part = slice(j * WEAVE, (j + 1) * WEAVE)
-        own = (o_keep[part] + wide(o_come[part]) * unit(o_scale[...])).astype(BF)
         slot_b = (b_keep[part] + wide(b_come[part]) * unit(b_scale[...])).astype(BF)
         one = jnp.where(place == 0, zero, jnp.where(place == 3, r_b[part], slot_b))
         two = jnp.where(place >= 2, r_a[part], zero)
         three = jnp.where(place == 3, slot_b, zero)
-        rows = jnp.concatenate([own, one, two, three], axis=0)
+        rows = jnp.concatenate([o_done[part], one, two, three], axis=0)
         out[part] = jnp.dot(mix[...], rows, preferred_element_type=F32).astype(BF).reshape(WEAVE, LAYERS, width)
 
 
-def weave(idx, o_keep, o_come, b_keep, b_come, r_a, r_b):
-    f, width = o_keep.shape
-    tile = 256
+def weave(idx, o_done, b_keep, b_come, r_a, r_b):
+    f, width = o_done.shape
+    tile = 512
     block = pl.BlockSpec((tile, width), lambda i, s: (i, 0))
     scale = pl.BlockSpec((SCALE_ROWS, width), lambda i, s: (f // SCALE_ROWS, 0))
     return pl.pallas_call(
@@ -380,14 +386,14 @@
         grid_spec=pltpu.PrefetchScalarGridSpec(
             num_scalar_prefetch=1,
             grid=(f // tile,),
-            in_specs=[block, block, scale, block, block, scale, block, block],
+            in_specs=[block, block, block, scale, block, block],
             out_specs=pl.BlockSpec((tile, LAYERS, width), lambda i, s: (i, 0, 0)),
             scratch_shapes=[pltpu.VMEM((LAYERS * WEAVE, LAYERS * WEAVE), BF)],
         ),
         out_shape=jax.ShapeDtypeStruct((f, LAYERS, width), BF),
         compiler_params=params(36),
         cost_estimate=cost(2 * f * LAYERS * 256 * width, 8 << 20),
-    )(idx, o_keep, o_come, o_come, b_keep, b_come, b_come, r_a, r_b)
+    )(idx, o_done, b_keep, b_come, b_come, r_a, r_b)
 
 
 def moved(array, group, pairs):
@@ -446,10 +452,10 @@
 
     b_code, b_left = more_terms(idx, near, far, own_e)
     b_come = swapped(b_code)
-    o_keep, b_keep, own_p = rest_terms(idx, high, low, b_left, own_e, w0)
+    o_done, b_keep, own_p = rest_terms(idx, high, low, b_left, own_e, w0, o_come)
 
     latent_grad = gated(mask, own_p, (one, two, three))
-    decoder_grad = weave(idx, o_keep, o_come, b_keep, b_come, r_a, r_b)
+    decoder_grad = weave(idx, o_done, b_keep, b_come, r_a, r_b)
     return decoder_grad, latent_grad
 
 

time: 110 us -> 112 us (1.018)
  the two profiles are of different devices: /device:TPU:38 before, /device:TPU:68 now
where the time goes in v4:
time: 112 us; the launch traced here: 111 us
  Pallas kernels  53.4 us (48%)
  waiting for transfers between devices  37.3 us (33%)
  starting transfers between devices  15.8 us (14%)
  local copies, waits for them, and re-layouts  4.05 us (4%)
    ppermute x3, waiting for transfers between devices, swapped(): return lax.ppermute(array, 'tok', [(0, 1), (1, 0)])  24.9 us
    pallas_call x1, Pallas kernels, first_terms(): pl.pallas_call(first_kernel, name='first_terms', grid_spec=pltpu.Prefetch...  12.6 us
    ppermute x7, waiting for transfers between devices, moved(): lax.ppermute(array, 'dst', [(a * group + i, b * group + i) for a, b in pa...  12.4 us
    pallas_call x1, Pallas kernels, partials(): pl.pallas_call(partial_kernel, name='partials', grid_spec=pltpu.PrefetchS...  12.3 us
    pallas_call x1, Pallas kernels, rest_terms(): pl.pallas_call(rest_kernel, name='rest_terms', grid_spec=pltpu.PrefetchSc...  10 us
    ppermute x7, starting transfers between devices, moved(): lax.ppermute(array, 'dst', [(a * group + i, b * group + i) for a, b in pa...  8.98 us
    ppermute x3, starting transfers between devices, swapped(): return lax.ppermute(array, 'tok', [(0, 1), (1, 0)])  6.82 us
    pallas_call x1, Pallas kernels, more_terms(): pl.pallas_call(more_kernel, name='more_terms', grid_spec=pltpu.PrefetchSc...  4.5 us
  transfers between devices with their start and end apart: 10, of which 4 were waited for; matrix products, arithmetic and copies ran while one was open for 0% of the time, Pallas kernels for 33%

profile of v4, /device:TPU:68, one launch (start us, length us, event | category | flops | bytes accessed | tf_op | source)
XLA Modules:
  0.0 111.4 jit_solution(9702145117770615692)
XLA Ops:
  0.6 0.1 pad_add_fusion.idx
  0.7 12.6 %first_terms.1 = (bf16[1024,2048]{1,0:T(8,128)(2,1)S(1)}, bf16[1024,1024]{1,0:T(8,128)(2,1)}, bf16[512,1024]{1,0:T(8,128)(2,1)}, bf16[512,1024]{1,0:T(8,128)(2,1...) custom-call(s32[3]{0:T(128)S(1)} %pad_add_fusion.idx, bf16[1024,4,2048]{2,1,0:T(4,128)(2,1)} %er.1, ...), custom_call_target="tpu_custom_call" | custom-call | flops 17179869184 | bytes 31457280 | tf_op jit(solution)/shard_map/first_terms/pallas_call | solution.py:112
  13.3 0.7 collective-permute-start.1
  14.1 1.3 %collective-permute-start = (s16[1032,512]{1,0:T(8,128)(2,1)S(1)}, s16[1032,512]{1,0:T(8,128)(2,1)S(1)}, u32[]{:S(2)}, u32[]{:S(2)}) collective-permute-start(s16[1032,512]{1,0:T(8,128)(2,1)S(1)} %get-tuple-element.19), channel_id=1, source_target_pairs={{0,32},{2,34},{4,36},{6,38},{8,40},{10,42},{12,44},{14,46},{16,48}... | collective-permute-start | bytes 3170312 | tf_op jit(solution)/shard_map/ppermute | solution.py:400
  15.4 1.2 %copy-done.3 = bf16[512,1024]{1,0:T(8,128)(2,1)S(1)} copy-done((bf16[512,1024]{1,0:T(8,128)(2,1)S(1)}, bf16[512,1024]{1,0:T(8,128)(2,1)}, u32[]{:S(2)}) %copy-start.3) | copy-done | bytes 1048600
  16.6 1.2 %copy-done.6 = bf16[512,1024]{1,0:T(8,128)(2,1)S(1)} copy-done((bf16[512,1024]{1,0:T(8,128)(2,1)S(1)}, bf16[512,1024]{1,0:T(8,128)(2,1)}, u32[]{:S(2)}) %copy-start.6) | copy-done | bytes 1048600
  17.8 3.8 %own_terms.1 = s16[520,1024]{1,0:T(8,128)(2,1)S(1)} custom-call(s32[3]{0:T(128)S(1)} %pad_add_fusion.idx, bf16[512,1024]{1,0:T(8,128)(2,1)S(1)} %copy-done.3, bf16[512,1024]{1,0:T(8,128)(2,1)S(1)} %copy-done.6, bf16[1024,2048]{1,0:T(8,128)(2,1)S(1)} %get-tuple-element.20.e), custom_call_target="tpu_custom_call" | custom-call | flops 2147483648 | bytes 6291456 | tf_op jit(solution)/shard_map/own_terms/pallas_call | solution.py:159
  21.6 3.3 %collective-permute-start.2 = (s16[520,1024]{1,0:T(8,128)(2,1)S(1)}, s16[520,1024]{1,0:T(8,128)(2,1)S(1)}, u32[]{:S(2)}, u32[]{:S(2)}) collective-permute-start(s16[520,1024]{1,0:T(8,128)(2,1)S(1)} %own_terms.1), channel_id=1, source_target_pairs={{0,1},{1,0},{2,3},{3,2},{4,5},{5,4},{6,7},{7,6},{8,9},{9,8},{10,11... | collective-permute-start | bytes 3194888 | tf_op jit(solution)/shard_map/ppermute | solution.py:404
  24.9 0.4 collective-permute-start.4
  25.3 12.3 %partials.1 = (bf16[512,2048]{1,0:T(8,128)(2,1)}, s16[1032,512]{1,0:T(8,128)(2,1)S(1)}, s16[1032,512]{1,0:T(8,128)(2,1)S(1)}, s16[1032,512]{1,0:T(8,128)(2,1)S(1)}) custom-call(s32[3]{0:T(128)S(1)} %pad_add_fusion.idx, bf16[1024,2048]{1,0:T(8,128)(2,1)S(1)} %get-tuple-element.20.e, bf16[512,4,2048]{2,1,0:T(4,128)(2,1)} %w.1), custom_call_target="tpu_custom_call" | custom-call | flops 8589934592 | bytes 20971520 | tf_op jit(solution)/shard_map/partials/pallas_call | solution.py:332
  37.6 1.9 %collective-permute-start.7 = (s16[1032,512]{1,0:T(8,128)(2,1)S(1)}, s16[1032,512]{1,0:T(8,128)(2,1)S(1)}, u32[]{:S(2)}, u32[]{:S(2)}) collective-permute-start(s16[1032,512]{1,0:T(8,128)(2,1)S(1)} %get-tuple-element.29), channel_id=1, source_target_pairs={{96,64},{98,66},{100,68},{102,70},{104,72},{106,74},{108,76},{110,... | collective-permute-start | bytes 3170312 | tf_op jit(solution)/shard_map/ppermute | solution.py:400
  39.5 0.0 collective-permute-done.1.far
  39.5 1.4 %collective-permute-start.8 = (s16[1032,512]{1,0:T(8,128)(2,1)S(1)}, s16[1032,512]{1,0:T(8,128)(2,1)S(1)}, u32[]{:S(2)}, u32[]{:S(2)}) collective-permute-start(s16[1032,512]{1,0:T(8,128)(2,1)S(1)} %get-tuple-element.30), channel_id=1, source_target_pairs={{96,32},{98,34},{100,36},{102,38},{104,40},{106,42},{108,44},{110,... | collective-permute-start | bytes 3170312 | tf_op jit(solution)/shard_map/ppermute | solution.py:400
  40.9 0.2 collective-permute-done.near
  41.0 0.8 collective-permute-start.9
  41.9 4.5 %more_terms.1 = (s16[520,1024]{1,0:T(8,128)(2,1)S(1)}, bf16[512,2048]{1,0:T(8,128)(2,1)S(1)}) custom-call(s32[3]{0:T(128)S(1)} %pad_add_fusion.idx, s16[1032,512]{1,0:T(8,128)(2,1)S(1)} %collective-permute-done.near, s16[1032,512]{1,0:T(8,128)(2,1)S(1)} %collective-permute-done.1.far, bf16[1024,2048]{1,0:T(8,128)(2,1)S(1)} %get-tuple-element.20.e), custom_call_target="tpu_custom_call" | custom-call | flops 2147483648 | bytes 8388608 | tf_op jit(solution)/shard_map/more_terms/pallas_call | solution.py:194
  46.4 24.9 %collective-permute-done.4.come.scale = s16[520,1024]{1,0:T(8,128)(2,1)S(1)} collective-permute-done((s16[520,1024]{1,0:T(8,128)(2,1)S(1)}, s16[520,1024]{1,0:T(8,128)(2,1)S(1)}, u32[]{:S(2)}, u32[]{:S(2)}) %collective-permute-start.4) | collective-permute-done | bytes 1064992 | tf_op jit(solution)/shard_map/ppermute | solution.py:404
  71.3 3.2 %collective-permute-start.3 = (s16[520,1024]{1,0:T(8,128)(2,1)S(1)}, s16[520,1024]{1,0:T(8,128)(2,1)S(1)}, u32[]{:S(2)}, u32[]{:S(2)}) collective-permute-start(s16[520,1024]{1,0:T(8,128)(2,1)S(1)} %get-tuple-element.25), channel_id=1, source_target_pairs={{0,1},{1,0},{2,3},{3,2},{4,5},{5,4},{6,7},{7,6},{8,9},{9,8},{10,11... | collective-permute-start | bytes 3194888 | tf_op jit(solution)/shard_map/ppermute | solution.py:404
  74.5 4.2 %join.1 = bf16[512,1024]{1,0:T(8,128)(2,1)} custom-call(s32[3]{0:T(128)S(1)} %pad_add_fusion.idx, bf16[512,1024]{1,0:T(8,128)(2,1)S(1)} %copy-done.4, bf16[512,1024]{1,0:T(8,128)(2,1)S(1)} %copy-done.7, bf16[1024,1024]{1,0:T(8,128)(2,1)S(1)} %copy-done.2, s16[520,1024]{1,0:T(8,128)(2,1)S(1)} %collective-permute-done.4.come.scale, ...), custom_call_target="tpu_custom_call" | custom-call | flops 2147483648 | bytes 6291456 | tf_op jit(solution)/shard_map/join/pallas_call | solution.py:279
  78.7 0.0 collective-permute-done.7.one.one_scale
  78.7 1.3 %collective-permute-start.6 = (bf16[512,1024]{1,0:T(8,128)(2,1)}, bf16[512,1024]{1,0:T(8,128)(2,1)S(1)}, u32[]{:S(2)}, u32[]{:S(2)}) collective-permute-start(bf16[512,1024]{1,0:T(8,128)(2,1)} %join.1), channel_id=1, source_target_pairs={{64,96},{66,98},{68,100},{70,102},{72,104},{74,106},{76,108},{78,1... | collective-permute-start | bytes 3145736 | tf_op jit(solution)/shard_map/ppermute | solution.py:400
  80.1 0.0 collective-permute-done.2.o_come.o_scale
  80.1 1.5 %collective-permute-start.5 = (bf16[512,1024]{1,0:T(8,128)(2,1)}, bf16[512,1024]{1,0:T(8,128)(2,1)S(1)}, u32[]{:S(2)}, u32[]{:S(2)}) collective-permute-start(bf16[512,1024]{1,0:T(8,128)(2,1)} %join.1), channel_id=1, source_target_pairs={{0,64},{2,66},{4,68},{6,70},{8,72},{10,74},{12,76},{14,78},{16,80}... | collective-permute-start | bytes 3145736 | tf_op jit(solution)/shard_map/ppermute | solution.py:400
  81.6 1.6 %copy-done.9 = bf16[512,2048]{1,0:T(8,128)(2,1)S(1)} copy-done((bf16[512,2048]{1,0:T(8,128)(2,1)S(1)}, bf16[512,2048]{1,0:T(8,128)(2,1)}, u32[]{:S(2)}) %copy-start.9) | copy-done | bytes 2097176
  83.2 10.0 %rest_terms.1 = (bf16[512,1024]{1,0:T(8,128)(2,1)S(1)}, f32[512,1024]{1,0:T(8,128)S(1)}, f32[1024,512]{1,0:T(8,128)S(1)}) custom-call(s32[3]{0:T(128)S(1)} %pad_add_fusion.idx, bf16[512,1024]{1,0:T(8,128)(2,1)S(1)} %copy-done.5, bf16[512,1024]{1,0:T(8,128)(2,1)S(1)} %copy-done.8, bf16[512,2048]{1,0:T(8,128)(2,1)S(1)} %get-tuple-element.21.b_left, ...), custom_call_target="tpu_custom_call" | custom-call | flops 6442450944 | bytes 16777216 | tf_op jit(solution)/shard_map/rest_terms/pallas_call | solution.py:238
  93.2 0.0 collective-permute-done.8.two.two_scale
  93.2 0.0 collective-permute-done.9.three.three_scale
  93.3 2.0 %gate.1 = f32[1024,512]{1,0:T(8,128)} custom-call(s32[1024,512]{1,0:T(8,128)S(1)} %copy-done, f32[1024,512]{1,0:T(8,128)S(1)} %get-tuple-element.28.own, s16[1032,512]{1,0:T(8,128)(2,1)S(1)} %collective-permute-done.7.one.one_scale, s16[1032,512]{1,0:T(8,128)(2,1)S(1)} %collective-permute-done.8.two.two_scale, ...), custom_call_target="tpu_custom_call" | custom-call | flops 4194304 | bytes 9437184 | tf_op jit(solution)/shard_map/gate/pallas_call | solution.py:419
  95.2 6.6 %collective-permute-done.6.r_b = bf16[512,1024]{1,0:T(8,128)(2,1)S(1)} collective-permute-done((bf16[512,1024]{1,0:T(8,128)(2,1)}, bf16[512,1024]{1,0:T(8,128)(2,1)S(1)}, u32[]{:S(2)}, u32[]{:S(2)}) %collective-permute-start.6) | collective-permute-done | bytes 1048608 | tf_op jit(solution)/shard_map/ppermute | solution.py:400
  101.9 5.6 %collective-permute-done.5.r_a = bf16[512,1024]{1,0:T(8,128)(2,1)S(1)} collective-permute-done((bf16[512,1024]{1,0:T(8,128)(2,1)}, bf16[512,1024]{1,0:T(8,128)(2,1)S(1)}, u32[]{:S(2)}, u32[]{:S(2)}) %collective-permute-start.5) | collective-permute-done | bytes 1048608 | tf_op jit(solution)/shard_map/ppermute | solution.py:400
  107.5 0.0 collective-permute-done.3.b_come.b_scale
  107.5 3.9 %weave.1 = bf16[512,4,1024]{2,1,0:T(4,128)(2,1)} custom-call(s32[3]{0:T(128)S(1)} %pad_add_fusion.idx, bf16[512,1024]{1,0:T(8,128)(2,1)S(1)} %get-tuple-element.23.o_done, f32[512,1024]{1,0:T(8,128)S(1)} %get-tuple-element.24.b_keep, s16[520,1024]{1,0:T(8,128)(2,1)S(1)} %collective-permute-done.3.b_come.b_scale, ...), custom_call_target="tpu_custom_call" | custom-call | flops 1073741824 | bytes 8388608 | tf_op jit(solution)/shard_map/weave/pallas_call | solution.py:383
  (17 shorter events, 0.0 us)
Async XLA Ops:
  13.3 28.5 %copy-start.1 = (bf16[1024,2048]{1,0:T(8,128)(2,1)}, bf16[1024,2048]{1,0:T(8,128)(2,1)S(1)}, u32[]{:S(2)}) copy-start(bf16[1024,2048]{1,0:T(8,128)(2,1)S(1)} %get-tuple-element.20.e) | copy-start | bytes 12582916
  13.3 26.1 %collective-permute-start.1 = (s16[1032,512]{1,0:T(8,128)(2,1)S(1)}, s16[1032,512]{1,0:T(8,128)(2,1)S(1)}, u32[]{:S(2)}, u32[]{:S(2)}) collective-permute-start(s16[1032,512]{1,0:T(8,128)(2,1)S(1)} %get-tuple-element.19), channel_id=1, source_target_pairs={{0,96},{2,98},{4,100},{6,102},{8,104},{10,106},{12,108},{14,110},{... | collective-permute-start | bytes 3170312 | tf_op jit(solution)/shard_map/ppermute | solution.py:400
  14.1 27.0 %collective-permute-start = (s16[1032,512]{1,0:T(8,128)(2,1)S(1)}, s16[1032,512]{1,0:T(8,128)(2,1)S(1)}, u32[]{:S(2)}, u32[]{:S(2)}) collective-permute-start(s16[1032,512]{1,0:T(8,128)(2,1)S(1)} %get-tuple-element.19), channel_id=1, source_target_pairs={{0,32},{2,34},{4,36},{6,38},{8,40},{10,42},{12,44},{14,46},{16,48}... | collective-permute-start | bytes 3170312 | tf_op jit(solution)/shard_map/ppermute | solution.py:400
  15.4 1.2 %copy-start.3 = (bf16[512,1024]{1,0:T(8,128)(2,1)S(1)}, bf16[512,1024]{1,0:T(8,128)(2,1)}, u32[]{:S(2)}) copy-start(bf16[512,1024]{1,0:T(8,128)(2,1)} %get-tuple-element.17.high) | copy-start | bytes 3145732
  16.6 1.2 %copy-start.6 = (bf16[512,1024]{1,0:T(8,128)(2,1)S(1)}, bf16[512,1024]{1,0:T(8,128)(2,1)}, u32[]{:S(2)}) copy-start(bf16[512,1024]{1,0:T(8,128)(2,1)} %get-tuple-element.18.low) | copy-start | bytes 3145732
  21.6 58.4 %collective-permute-start.2 = (s16[520,1024]{1,0:T(8,128)(2,1)S(1)}, s16[520,1024]{1,0:T(8,128)(2,1)S(1)}, u32[]{:S(2)}, u32[]{:S(2)}) collective-permute-start(s16[520,1024]{1,0:T(8,128)(2,1)S(1)} %own_terms.1), channel_id=1, source_target_pairs={{0,1},{1,0},{2,3},{3,2},{4,5},{5,4},{6,7},{7,6},{8,9},{9,8},{10,11... | collective-permute-start | bytes 3194888 | tf_op jit(solution)/shard_map/ppermute | solution.py:404
  24.9 46.4 %collective-permute-start.4 = (s16[520,1024]{1,0:T(8,128)(2,1)S(1)}, s16[520,1024]{1,0:T(8,128)(2,1)S(1)}, u32[]{:S(2)}, u32[]{:S(2)}) collective-permute-start(s16[520,1024]{1,0:T(8,128)(2,1)S(1)} %get-tuple-element.27), channel_id=1, source_target_pairs={{0,1},{1,0},{2,3},{3,2},{4,5},{5,4},{6,7},{7,6},{8,9},{9,8},{10,11... | collective-permute-start | bytes 3194888 | tf_op jit(solution)/shard_map/ppermute | solution.py:404
  37.6 41.1 %collective-permute-start.7 = (s16[1032,512]{1,0:T(8,128)(2,1)S(1)}, s16[1032,512]{1,0:T(8,128)(2,1)S(1)}, u32[]{:S(2)}, u32[]{:S(2)}) collective-permute-start(s16[1032,512]{1,0:T(8,128)(2,1)S(1)} %get-tuple-element.29), channel_id=1, source_target_pairs={{96,64},{98,66},{100,68},{102,70},{104,72},{106,74},{108,76},{110,... | collective-permute-start | bytes 3170312 | tf_op jit(solution)/shard_map/ppermute | solution.py:400
  39.5 53.7 %collective-permute-start.8 = (s16[1032,512]{1,0:T(8,128)(2,1)S(1)}, s16[1032,512]{1,0:T(8,128)(2,1)S(1)}, u32[]{:S(2)}, u32[]{:S(2)}) collective-permute-start(s16[1032,512]{1,0:T(8,128)(2,1)S(1)} %get-tuple-element.30), channel_id=1, source_target_pairs={{96,32},{98,34},{100,36},{102,38},{104,40},{106,42},{108,44},{110,... | collective-permute-start | bytes 3170312 | tf_op jit(solution)/shard_map/ppermute | solution.py:400
  41.0 33.5 %copy-start.2 = (bf16[1024,1024]{1,0:T(8,128)(2,1)S(1)}, bf16[1024,1024]{1,0:T(8,128)(2,1)}, u32[]{:S(2)}) copy-start(bf16[1024,1024]{1,0:T(8,128)(2,1)} %get-tuple-element.26.e) | copy-start | bytes 6291460
  41.0 33.5 %copy-start.4 = (bf16[512,1024]{1,0:T(8,128)(2,1)S(1)}, bf16[512,1024]{1,0:T(8,128)(2,1)}, u32[]{:S(2)}) copy-start(bf16[512,1024]{1,0:T(8,128)(2,1)} %get-tuple-element.17.high) | copy-start | bytes 3145732
  41.0 33.5 %copy-start.7 = (bf16[512,1024]{1,0:T(8,128)(2,1)S(1)}, bf16[512,1024]{1,0:T(8,128)(2,1)}, u32[]{:S(2)}) copy-start(bf16[512,1024]{1,0:T(8,128)(2,1)} %get-tuple-element.18.low) | copy-start | bytes 3145732
  41.0 52.2 %collective-permute-start.9 = (s16[1032,512]{1,0:T(8,128)(2,1)S(1)}, s16[1032,512]{1,0:T(8,128)(2,1)S(1)}, u32[]{:S(2)}, u32[]{:S(2)}) collective-permute-start(s16[1032,512]{1,0:T(8,128)(2,1)S(1)} %get-tuple-element.31), channel_id=1, source_target_pairs={{96,0},{98,2},{100,4},{102,6},{104,8},{106,10},{108,12},{110,14},{... | collective-permute-start | bytes 3170312 | tf_op jit(solution)/shard_map/ppermute | solution.py:400
  71.3 36.2 %collective-permute-start.3 = (s16[520,1024]{1,0:T(8,128)(2,1)S(1)}, s16[520,1024]{1,0:T(8,128)(2,1)S(1)}, u32[]{:S(2)}, u32[]{:S(2)}) collective-permute-start(s16[520,1024]{1,0:T(8,128)(2,1)S(1)} %get-tuple-element.25), channel_id=1, source_target_pairs={{0,1},{1,0},{2,3},{3,2},{4,5},{5,4},{6,7},{7,6},{8,9},{9,8},{10,11... | collective-permute-start | bytes 3194888 | tf_op jit(solution)/shard_map/ppermute | solution.py:404
  74.5 7.1 %copy-start.5 = (bf16[512,1024]{1,0:T(8,128)(2,1)S(1)}, bf16[512,1024]{1,0:T(8,128)(2,1)}, u32[]{:S(2)}) copy-start(bf16[512,1024]{1,0:T(8,128)(2,1)} %get-tuple-element.17.high) | copy-start | bytes 3145732
  74.5 7.1 %copy-start.8 = (bf16[512,1024]{1,0:T(8,128)(2,1)S(1)}, bf16[512,1024]{1,0:T(8,128)(2,1)}, u32[]{:S(2)}) copy-start(bf16[512,1024]{1,0:T(8,128)(2,1)} %get-tuple-element.18.low) | copy-start | bytes 3145732
  78.7 23.2 %collective-permute-start.6 = (bf16[512,1024]{1,0:T(8,128)(2,1)}, bf16[512,1024]{1,0:T(8,128)(2,1)S(1)}, u32[]{:S(2)}, u32[]{:S(2)}) collective-permute-start(bf16[512,1024]{1,0:T(8,128)(2,1)} %join.1), channel_id=1, source_target_pairs={{64,96},{66,98},{68,100},{70,102},{72,104},{74,106},{76,108},{78,1... | collective-permute-start | bytes 3145736 | tf_op jit(solution)/shard_map/ppermute | solution.py:400
  80.1 27.4 %collective-permute-start.5 = (bf16[512,1024]{1,0:T(8,128)(2,1)}, bf16[512,1024]{1,0:T(8,128)(2,1)S(1)}, u32[]{:S(2)}, u32[]{:S(2)}) collective-permute-start(bf16[512,1024]{1,0:T(8,128)(2,1)} %join.1), channel_id=1, source_target_pairs={{0,64},{2,66},{4,68},{6,70},{8,72},{10,74},{12,76},{14,78},{16,80}... | collective-permute-start | bytes 3145736 | tf_op jit(solution)/shard_map/ppermute | solution.py:400
  81.6 1.6 %copy-start.9 = (bf16[512,2048]{1,0:T(8,128)(2,1)S(1)}, bf16[512,2048]{1,0:T(8,128)(2,1)}, u32[]{:S(2)}) copy-start(bf16[512,2048]{1,0:T(8,128)(2,1)} %get-tuple-element.22.w0) | copy-start | bytes 6291460
  83.2 10.1 %copy-start = (s32[1024,512]{1,0:T(8,128)S(1)}, s32[1024,512]{1,0:T(8,128)}, u32[]{:S(2)}) copy-start(s32[1024,512]{1,0:T(8,128)} %mask.1) | copy-start | bytes 6291460
